TPU v7x, 768 devices: a whole 4x8x12 slice. The times are simulated.
768 devices in a mesh: dp: 64 (over x, y, core), tensor: 12 (over z).
Axes of the slice: x: 4, y: 8, z: 12, core: 2. Of those that a mesh axis runs over, the one named last changes fastest.
Arguments:
- image_rows: bfloat16 [32768, 3072], P('dp'), may hold values from -6 to 6
- image_mod: float32 [64, 2, 3072], P('dp'), may hold values from -3 to 3
- caption_rows: bfloat16 [16384, 3072], P('dp'), may hold values from -6 to 6
- caption_mod: float32 [64, 2, 3072], replicated, may hold values from -3 to 3
- row_owner: int32 [16384, 1], P('dp'), may hold values from 0 to 63; in each aligned block of 256 rows (0 to 255, 256 to 511, ...) at most 8 rows name the same one
- w_img_qkv: bfloat16 [3072, 3, 3072], P('dp', None, 'tensor'), may hold values from -0.109375 to 0.109375
- w_txt_qkv: bfloat16 [3072, 3, 3072], P('dp', None, 'tensor'), may hold values from -0.109375 to 0.109375
- img_qk_gain: float32 [2, 128], replicated, may hold values from 0.5 to 3
- txt_qk_gain: float32 [2, 128], replicated, may hold values from 0.5 to 3
Outputs:
- image_attn: bfloat16 [32768, 3072], P('dp', 'tensor')
- caption_attn: bfloat16 [16384, 3072], P('dp', 'tensor')
Inputs may be any that keep to these rules, and one draw needn't show every extreme that they name: `row_owner`: among the 256 caption tokens of one bin (aligned blocks of rows), no sample is named more than 8 times, a bound that some block reaches.
All inputs are finite; a program needn't handle non-finite values.
Results may differ from a plain program's by a relative error of at most 0.012.
The roundings to bfloat16 on the way count: a program that leaves them out, or rounds other values in their place, can miss the bound.
Values may be sent and summed in bfloat16 or wider, within the bound.
A program may use at most 64 MiB of HBM per device.

v0:
```python
import math

import jax
import jax.numpy as jnp
from jax import lax
from jax.sharding import PartitionSpec as P

HD = 128


def layer_norm(rows):
    values = rows.astype(jnp.float32)
    mean = jnp.mean(values, axis=-1, keepdims=True)
    var = jnp.mean((values - mean) ** 2, axis=-1, keepdims=True)
    return (values - mean) * lax.rsqrt(var + 1e-06)


def head_norm(values, gain):
    return values * lax.rsqrt(jnp.mean(values * values, axis=-1, keepdims=True) + 1e-06) * gain


def add_rows(left, piece):
    return jnp.dot(left, piece.reshape(piece.shape[0], -1), preferred_element_type=jnp.float32)


def split_heads(qkv, gain, heads_dev):
    qkv = qkv.reshape(qkv.shape[0], 3, heads_dev, HD)
    query = head_norm(qkv[:, 0], gain[0]).astype(jnp.bfloat16)
    keys = head_norm(qkv[:, 1], gain[1]).astype(jnp.bfloat16)
    return (query, keys, qkv[:, 2].astype(jnp.bfloat16))


def body(
    image_rows,
    image_mod,
    caption_rows,
    caption_mod,
    row_owner,
    w_img_qkv,
    w_txt_qkv,
    img_qk_gain,
    txt_qk_gain,
):
    n_dp = lax.axis_size("dp")
    bin_rows = caption_rows.shape[0]
    img_rows = image_rows.shape[0]
    width = caption_rows.shape[1]
    cols_dev = w_img_qkv.shape[2]
    heads_dev = cols_dev // HD
    slot = 2 * bin_rows // n_dp
    img_in = (layer_norm(image_rows) * (1.0 + image_mod[0, 1]) + image_mod[0, 0]).astype(
        jnp.bfloat16
    )
    owner = row_owner[:, 0]
    picks = owner[:, None] == jnp.arange(n_dp, dtype=jnp.int32)[None, :]
    onehot = picks.astype(jnp.float32)
    mods = jnp.dot(onehot, caption_mod.reshape(n_dp, 2 * width), precision=lax.Precision.HIGHEST)
    txt_in = (layer_norm(caption_rows) * (1.0 + mods[:, width:]) + mods[:, :width]).astype(
        jnp.bfloat16
    )
    txt_qkv = add_rows(txt_in, lax.all_gather(w_txt_qkv, "dp", axis=0, tiled=True))
    img_qkv = add_rows(img_in, lax.all_gather(w_img_qkv, "dp", axis=0, tiled=True))
    iq, ik, iv = split_heads(img_qkv, img_qk_gain, heads_dev)
    tq, tk, tv = split_heads(txt_qkv, txt_qk_gain, heads_dev)
    payload = jnp.stack([tq, tk, tv], axis=1).reshape(bin_rows, 3 * cols_dev)
    marks = picks.astype(jnp.int32)
    before = jnp.cumsum(marks, axis=0) - marks
    position = jnp.sum(before * marks, axis=1)
    target = owner * slot + position
    outgoing = (
        jnp.zeros((n_dp * slot, 3 * cols_dev), jnp.bfloat16)
        .at[target]
        .set(payload)
        .reshape(n_dp, slot, 3 * cols_dev)
    )
    present = (
        jnp.zeros((n_dp * slot,), jnp.bfloat16)
        .at[target]
        .set(jnp.ones((bin_rows,), jnp.bfloat16))
        .reshape(n_dp, slot)
    )
    arrived, arrived_live = (
        lax.all_to_all(outgoing, "dp", split_axis=0, concat_axis=0, tiled=True),
        lax.all_to_all(present, "dp", split_axis=0, concat_axis=0, tiled=True),
    )
    caption_heads = arrived.reshape(n_dp * slot, 3, heads_dev, HD)
    query = jnp.concatenate([caption_heads[:, 0], iq], axis=0)
    keys = jnp.concatenate([caption_heads[:, 1], ik], axis=0)
    values = jnp.concatenate([caption_heads[:, 2], iv], axis=0)
    live = jnp.concatenate([arrived_live.reshape(-1) > 0.5, jnp.ones((img_rows,), bool)])
    scores = jnp.einsum(
        "qhd,khd->hqk", query, keys, preferred_element_type=jnp.float32
    ) / math.sqrt(HD)
    scores = jnp.where(live[None, None, :], scores, -jnp.inf)
    weights = jax.nn.softmax(scores, axis=-1).astype(jnp.bfloat16)
    result = jnp.einsum("hqk,khd->qhd", weights, values, preferred_element_type=jnp.float32).astype(
        jnp.bfloat16
    )
    image_attn = result[n_dp * slot :].reshape(img_rows, cols_dev)
    caption_back = result[: n_dp * slot].reshape(n_dp, slot, cols_dev)
    returned = lax.all_to_all(caption_back, "dp", split_axis=0, concat_axis=0, tiled=True).reshape(
        n_dp * slot, cols_dev
    )
    caption_attn = returned[target]
    return (image_attn, caption_attn)


def solution(mesh):
    in_specs = (
        P("dp", None),
        P("dp", None, None),
        P("dp", None),
        P(),
        P("dp", None),
        P("dp", None, "tensor"),
        P("dp", None, "tensor"),
        P(),
        P(),
    )
    out_specs = (P("dp", "tensor"), P("dp", "tensor"))
    return jax.shard_map(body, mesh=mesh, in_specs=in_specs, out_specs=out_specs, check_vma=False)
```

profile of v0, /device:TPU:1, one launch (start us, length us, event | category | flops | bytes accessed | tf_op | source)
XLA Modules:
  0.0 256.5 jit_solution(13709611921730607424)
XLA Ops:
  7.2 0.0 all-gather.3.cloned.1.call-start
  7.2 0.7 all-gather.3.cloned.1.call-update
  7.9 0.0 all-gather.5.cloned.1.call-start
  8.0 0.7 all-gather.5.cloned.1.call-update
  8.7 0.7 fusion.46
  9.4 0.6 reduce-window.6
  10.0 0.2 slice_reduce_fusion
  10.2 0.8 fusion.44
  11.0 0.7 compare_select_fusion
  11.7 2.2 scatter_custom_fusion.1
  13.8 0.7 all_to_all.16
  14.6 14.5 %all-to-all-start.1 = ((bf16[64,1,8]{2,1,0:T(2,128)(2,1)}), bf16[64,1,8]{2,1,0:T(2,128)(2,1)S(1)}, u32[]{:S(2)}, u32[]{:S(2)}) async-start(bf16[64,1,8]{2,1,0:T(2,128)(2,1)} %all_to_all.16), calls=%async_computation.1 | async-start | bytes 65536 | tf_op jit(solution)/shard_map/all_to_all | solution.py:84
  29.1 0.0 copy-start.1
  29.1 2.0 copy.46
  31.1 1.7 convert_reduce_fusion.1
  32.9 0.6 fusion.14
  33.4 0.6 slice_bitcast_fusion.3
  34.0 0.5 convert_reduce_fusion
  34.5 1.0 fusion.4
  35.5 0.6 add_rsqrt_fusion.2
  36.1 4.6 %fusion.45 = f32[256,6144]{1,0:T(8,128)} fusion(f32[64,6144]{1,0:T(8,128)S(1)} %bitcast.90, s32[256]{0:T(256)S(1)} %bitcast.102), kind=kOutput, calls=%fused_computation.77 | convolution fusion | flops 1207975936 | bytes 7865344 | tf_op jit(solution)/shard_map/dot_general | solution.py:57
  40.7 0.6 slice_add_fusion.1
  41.4 0.1 compare_reduce_fusion
  41.5 0.1 gt.11
  41.6 0.6 concatenate.13
  42.2 68.1 %all-gather.3.cloned.1.call-done = bf16[3072,3,256]{2,0,1:T(8,128)(2,1)} async-done(((bf16[48,3,256]{2,0,1:T(8,128)(2,1)}), bf16[3072,3,256]{2,0,1:T(8,128)(2,1)}) %all-gather.3.cloned.1.call-update) | async-done | bytes 4718608 | tf_op jit(solution)/shard_map/all_gather | solution.py:61
  110.3 6.6 %copy.27 = bf16[3072,3,256]{0,2,1:T(8,128)(2,1)} copy(bf16[3072,3,256]{2,0,1:T(8,128)(2,1)} %all-gather.3.cloned.1.call-done) | data formatting | bytes 9437184 | tf_op jit(solution)/shard_map/all_gather | solution.py:61
  116.9 6.2 %fusion.26 = f32[256,3,2,128]{0,3,2,1:T(8,128)S(1)} fusion(bf16[3,2,128,3072]{3,2,1,0:T(8,128)(2,1)} %bitcast.92, f32[256,6144]{1,0:T(8,128)} %fusion.45, bf16[256,3072]{1,0:T(8,128)(2,1)} %param.11, f32[256]{0:T(256)S(1)} %add_rsqrt_fusion.5, f32[256]{0:T(256)S(1)} %broadcast_multiply_fusion.1), kind=kOutput, calls=%fused_computation.36 | convolution fusion | flops 1213464576 | bytes 13371392 | tf_op jit(solution)/shard_map/dot_general | solution.py:23
  123.2 0.1 multiply_reduce_fusion.3
  123.3 0.1 multiply_convert_fusion.3
  123.4 0.9 copy.28
  124.4 3.0 %scatter_custom_fusion = bf16[512,768]{1,0:T(8,128)(2,1)} fusion(s32[256]{0:T(256)} %bitcast.107, bf16[256,768]{1,0:T(8,128)(2,1)} %copy.28, bf16[]{:T(256)} %constant.14.clone.1), kind=kCustom, calls=%fused_computation.56 | custom fusion | bytes 786944 | tf_op jit(solution)/shard_map/scatter | solution.py:73
  127.4 6.4 %all-to-all-start = ((bf16[64,8,768]{2,1,0:T(8,128)(2,1)}), bf16[64,8,768]{2,1,0:T(8,128)(2,1)}, u32[]{:S(2)}, u32[]{:S(2)}) async-start(bf16[64,8,768]{2,1,0:T(8,128)(2,1)} %bitcast.93), calls=%async_computation | async-start | bytes 1572864 | tf_op jit(solution)/shard_map/all_to_all | solution.py:83
  133.9 70.0 %all-gather.5.cloned.1.call-done = bf16[3072,3,256]{2,0,1:T(8,128)(2,1)} async-done(((bf16[48,3,256]{2,0,1:T(8,128)(2,1)}), bf16[3072,3,256]{2,0,1:T(8,128)(2,1)}) %all-gather.5.cloned.1.call-update) | async-done | bytes 4718608 | tf_op jit(solution)/shard_map/all_gather | solution.py:62
  203.9 6.6 %copy.30 = bf16[3072,3,256]{0,2,1:T(8,128)(2,1)} copy(bf16[3072,3,256]{2,0,1:T(8,128)(2,1)} %all-gather.5.cloned.1.call-done) | data formatting | bytes 9437184 | tf_op jit(solution)/shard_map/all_gather | solution.py:62
  210.5 5.4 %fusion.19 = f32[512,3,2,128]{3,0,2,1:T(8,128)S(1)} fusion(bf16[3,2,128,3072]{3,2,1,0:T(8,128)(2,1)} %bitcast.91, bf16[512,3072]{1,0:T(8,128)(2,1)S(1)} %copy-done, f32[3072]{0:T(1024)S(1)} %bitcast.104, f32[3072]{0:T(1024)S(1)} %bitcast.103, f32[512]{0:T(512)S(1)} %copy-done.9, f32[512]{0:T(512)S(1)} %broadcast_multiply_fusion), kind=kOutput, calls=%fused_computation.29 | convolution fusion | flops 2425356288 | bytes 9465856 | tf_op jit(solution)/shard_map/dot_general | solution.py:23
  215.9 0.4 multiply_reduce_fusion.1
  216.3 0.3 multiply_convert_fusion.1
  216.7 2.0 reshape.139
  218.7 0.5 fusion.58
  219.4 4.9 %fusion.60 = (f32[2,1024]{1,0:T(2,128)S(1)}, f32[2,1024,1024]{1,2,0:T(8,128)}) fusion(pred[1024]{0:T(1024)(128)(4,1)S(1)} %copy-done.12, bf16[512,2,128]{2,0,1:T(8,128)(2,1)S(1)} %get-tuple-element.13, bf16[512,2,128]{2,0,1:T(8,128)(2,1)S(1)} %bitcast.99, bf16[512,2,128]{2,0,1:T(8,128)(2,1)S(1)} %get-tuple-element.12, bf16[512,2,128]{2,0,1:T(8,128)(2,1)S(1)} %bitcast.98), kind=kOutput, calls=%fused_computation.105 | convolution fusion | flops 547357696 | bytes 9446400 | tf_op jit(solution)/shard_map/sub | solution.py:95
  224.4 4.2 %fusion.32 = bf16[1024,2,128]{0,2,1:T(8,128)(2,1)S(1)} fusion(f32[2,1024,1024]{1,2,0:T(8,128)} %get-tuple-element.28, f32[2,1024]{1,0:T(2,128)S(1)} %get-tuple-element.27, bf16[512,2,128]{2,0,1:T(8,128)(2,1)S(1)} %fusion.41, bf16[512,2,128]{2,0,1:T(8,128)(2,1)S(1)} %bitcast.97), kind=kOutput, calls=%fused_computation.41 | convolution fusion | flops 542375936 | bytes 9445376 | tf_op jit(solution)/shard_map/hqk,khd->qhd/dot_general | solution.py:96
  228.6 0.2 copy.36
  228.8 0.9 reshape.142
  229.6 6.2 %all-to-all-start.2 = ((bf16[64,8,256]{2,1,0:T(8,128)(2,1)}), bf16[64,8,256]{2,1,0:T(8,128)(2,1)S(1)}, u32[]{:S(2)}, u32[]{:S(2)}) async-start(bf16[64,8,256]{2,1,0:T(8,128)(2,1)} %reshape.142), calls=%async_computation.2 | async-start | bytes 524288 | tf_op jit(solution)/shard_map/all_to_all | solution.py:101
  235.9 0.8 copy.37
  236.8 11.1 %all-to-all-done.2 = bf16[64,8,256]{2,1,0:T(8,128)(2,1)S(1)} async-done(((bf16[64,8,256]{2,1,0:T(8,128)(2,1)}), bf16[64,8,256]{2,1,0:T(8,128)(2,1)S(1)}, u32[]{:S(2)}, u32[]{:S(2)}) %all-to-all-start.2) | async-done | bytes 262176 | tf_op jit(solution)/shard_map/all_to_all | solution.py:101
  247.9 1.8 gather_fusion
  (44 shorter events, 0.4 us)
Async XLA Ops:
  7.2 26.3 %copy-start.10 = (f32[2,128]{1,0:T(2,128)S(1)}, f32[2,128]{1,0:T(2,128)}, u32[]{:S(2)}) copy-start(f32[2,128]{1,0:T(2,128)} %param.16) | copy-start | bytes 3076
  7.2 26.8 %copy-start = (bf16[512,3072]{1,0:T(8,128)(2,1)S(1)}, bf16[512,3072]{1,0:T(8,128)(2,1)}, u32[]{:S(2)}) copy-start(bf16[512,3072]{1,0:T(8,128)(2,1)} %param.9) | copy-start | bytes 9437188
  7.2 103.1 %all-gather.3.cloned.1.call-start = ((), (), s32[]{:S(2)}) async-start(), calls=%async_computation.3 | async-start | bytes 4792320 | tf_op jit(solution)/shard_map/all_gather | solution.py:61
  7.9 195.9 %all-gather.5.cloned.1.call-start = ((), (), s32[]{:S(2)}) async-start(), calls=%async_computation.4 | async-start | bytes 4792320 | tf_op jit(solution)/shard_map/all_gather | solution.py:62
  11.7 2.9 %copy-start.5 = (s32[256,1]{0,1:T(1,128)}, s32[256,1]{0,1:T(1,128)S(1)}, u32[]{:S(2)}) copy-start(s32[256,1]{0,1:T(1,128)S(1)} %compare_select_fusion) | copy-start | bytes 3076
  14.6 26.8 %all-to-all-start.1 = ((bf16[64,1,8]{2,1,0:T(2,128)(2,1)}), bf16[64,1,8]{2,1,0:T(2,128)(2,1)S(1)}, u32[]{:S(2)}, u32[]{:S(2)}) async-start(bf16[64,1,8]{2,1,0:T(2,128)(2,1)} %all_to_all.16), calls=%async_computation.1 | async-start | bytes 65536 | tf_op jit(solution)/shard_map/all_to_all | solution.py:84
  29.1 3.7 %copy-start.1 = (bf16[256,3072]{1,0:T(8,128)(2,1)S(1)}, bf16[256,3072]{1,0:T(8,128)(2,1)}, u32[]{:S(2)}) copy-start(bf16[256,3072]{1,0:T(8,128)(2,1)} %param.11) | copy-start | bytes 4718596
  32.8 3.3 %copy-start.2 = (s32[256,1]{0,1:T(1,128)S(1)}, s32[256,1]{0,1:T(1,128)}, u32[]{:S(2)}) copy-start(s32[256,1]{0,1:T(1,128)} %param.13) | copy-start | bytes 3076
  35.5 5.3 %copy-start.3 = (f32[1,2,3072]{2,1,0:T(2,128)S(1)}, f32[1,2,3072]{2,1,0:T(2,128)}, u32[]{:S(2)}) copy-start(f32[1,2,3072]{2,1,0:T(2,128)} %param.10) | copy-start | bytes 73732
  35.5 5.9 %copy-start.11 = (f32[2,128]{1,0:T(2,128)S(1)}, f32[2,128]{1,0:T(2,128)}, u32[]{:S(2)}) copy-start(f32[2,128]{1,0:T(2,128)} %param.17) | copy-start | bytes 3076
  127.4 89.3 %all-to-all-start = ((bf16[64,8,768]{2,1,0:T(8,128)(2,1)}), bf16[64,8,768]{2,1,0:T(8,128)(2,1)}, u32[]{:S(2)}, u32[]{:S(2)}) async-start(bf16[64,8,768]{2,1,0:T(8,128)(2,1)} %bitcast.93), calls=%async_computation | async-start | bytes 1572864 | tf_op jit(solution)/shard_map/all_to_all | solution.py:83
  133.8 76.6 %copy-start.4 = (f32[1,1,3072]{2,1,0:T(1,128)S(1)}, f32[1,1,3072]{2,1,0:T(1,128)}, u32[]{:S(2)}) copy-start(f32[1,1,3072]{2,1,0:T(1,128)} %get-tuple-element.22) | copy-start | bytes 36868
  133.9 76.6 %copy-start.9 = (f32[512]{0:T(512)S(1)}, f32[512]{0:T(512)}, u32[]{:S(2)}) copy-start(f32[512]{0:T(512)} %add_rsqrt_fusion.2) | copy-start | bytes 6148
  210.5 5.8 %copy-start.7 = (f32[128]{0:T(128)S(1)}, f32[128]{0:T(128)}, u32[]{:S(2)}) copy-start(f32[128]{0:T(128)} %get-tuple-element.23) | copy-start | bytes 1540
  210.5 5.8 %copy-start.8 = (f32[128]{0:T(128)S(1)}, f32[128]{0:T(128)}, u32[]{:S(2)}) copy-start(f32[128]{0:T(128)} %get-tuple-element.24) | copy-start | bytes 1540
  215.9 3.5 %copy-start.12 = (pred[1024]{0:T(1024)(128)(4,1)S(1)}, pred[1024]{0:T(1024)(128)(4,1)}, u32[]{:S(2)}) copy-start(pred[1024]{0:T(1024)(128)(4,1)} %concatenate.13) | copy-start | bytes 3076
  224.4 11.5 %copy-start.6 = (s32[256,1]{0,1:T(1,128)S(1)}, s32[256,1]{0,1:T(1,128)}, u32[]{:S(2)}) copy-start(s32[256,1]{0,1:T(1,128)} %copy-done.5) | copy-start | bytes 3076
  229.6 18.3 %all-to-all-start.2 = ((bf16[64,8,256]{2,1,0:T(8,128)(2,1)}), bf16[64,8,256]{2,1,0:T(8,128)(2,1)S(1)}, u32[]{:S(2)}, u32[]{:S(2)}) async-start(bf16[64,8,256]{2,1,0:T(8,128)(2,1)} %reshape.142), calls=%async_computation.2 | async-start | bytes 524288 | tf_op jit(solution)/shard_map/all_to_all | solution.py:101
Sparse Core Ops, SparseCore 0:
  12.0 98.2 all-gather.2
  114.3 89.5 all-gather.4
where the time goes:
time: 257 us
  waiting for transfers between devices  151 us (59%)
  local copies, waits for them, and re-layouts  30.1 us (12%)
  starting transfers between devices  27.3 us (11%)
  matrix products  25.4 us (10%)
  between operations  14.4 us (6%)
  other arithmetic  8.79 us (3%)
    all_gather x1, waiting for transfers between devices, body(): lax.all_gather(w_img_qkv, 'dp', axis=0, tiled=True)  70 us
    all_gather x1, waiting for transfers between devices, body(): lax.all_gather(w_txt_qkv, 'dp', axis=0, tiled=True)  68.1 us
    all_to_all x1, starting transfers between devices, body(): lax.all_to_all(present, 'dp', split_axis=0, concat_axis=0, tiled=True)  14.5 us
    dot_general x2, matrix products, add_rows(): jnp.dot(left, piece.reshape(piece.shape[0], -1), preferred_element_type=j...  11.6 us
    all_to_all x1, waiting for transfers between devices, body(): lax.all_to_all(caption_back, 'dp', split_axis=0, concat_axis=0, tiled=True)  11.1 us
    all_gather x1, local copies, waits for them, and re-layouts, body(): lax.all_gather(w_txt_qkv, 'dp', axis=0, tiled=True)  6.63 us
    all_gather x1, local copies, waits for them, and re-layouts, body(): lax.all_gather(w_img_qkv, 'dp', axis=0, tiled=True)  6.62 us
    all_to_all x1, starting transfers between devices, body(): lax.all_to_all(outgoing, 'dp', split_axis=0, concat_axis=0, tiled=True)  6.42 us
  transfers between devices with their start and end apart: 5, of which 3 were waited for; matrix products, arithmetic and copies ran while one was open for 19% of the time, Pallas kernels for 0%

commit v1 on v0

v1 whole, which is shorter than its diff:
```python
import functools
import math

import jax
import jax.numpy as jnp
from jax import lax
from jax.experimental import pallas as pl
from jax.experimental.pallas import tpu as pltpu
from jax.sharding import PartitionSpec as P

MESH = pl.DeviceIdType.MESH
HD = 128
NX, NY, NC = 4, 8, 2
N_DP = NX * NY * NC
F32 = jnp.float32
BF16 = jnp.bfloat16


def kernel(
    img_hbm, imod_ref, cap_hbm, cmod_hbm, owner_ref, wimg_hbm, wtxt_hbm, igain_ref, tgain_ref,
    oimg_ref, ocap_ref,
    img_v, cap_v, cmod_v, mod3, modrow, img_in, txt_in, wt, wi, picks, counts_out, counts_in,
    proj, payload, out_buf, in_buf, qkv, ret_out, ret_in, bias,
    loc_sem, rsem, ssem, asem,
):
    dp = lax.axis_index("dp")
    x, y, c = dp // (NY * NC), (dp // NC) % NY, dp % NC

    def at(xx, yy, cc):
        return (xx * NY + yy) * NC + cc

    def xs(d):
        return (x + d + NX) % NX

    def ys(d):
        return (y + d + NY) % NY

    dev = {
        "x+": at(xs(1), y, c), "x-": at(xs(-1), y, c),
        "y+": at(x, ys(1), c), "y-": at(x, ys(-1), c),
        "p": at(x, y, 1 - c),
    }
    weights = (wt, wi)

    loads = []
    for i, (src, dst) in enumerate((
        (wtxt_hbm, wt.at[x, y, c]), (wimg_hbm, wi.at[x, y, c]),
        (cmod_hbm, cmod_v), (cap_hbm, cap_v), (img_hbm, img_v),
    )):
        copy = pltpu.make_async_copy(src, dst, loc_sem.at[i])
        copy.start()
        loads.append(copy)

    barrier = pltpu.get_barrier_semaphore()
    for d in dev.values():
        pl.semaphore_signal(barrier, inc=1, device_id={"dp": d}, device_id_type=MESH)

    def ypiece(t, xx, yy):
        return weights[t].at[xx, yy, c, :, 16:48, :]

    def yhalf(t, xx, yy, h):
        return weights[t].at[xx, yy, c, :, 16 + 16 * h : 32 + 16 * h, :]

    def xpiece(t, xx, yy):
        return weights[t].at[xx, yy, c, :, 0:16, :]

    def xrow(t, yy, h):
        return weights[t].at[2 * h : 2 * h + 2, yy, c, :, 0:16, :]

    def ycol(t, xx):
        return weights[t].at[xx, :, c, :, 16:48, :]

    def ycolhalf(t, xx, h):
        return weights[t].at[xx, 4 * h : 4 * h + 4, c, :, 16:48, :]

    sent = []
    n_sent = [0, 0]
    names = {}

    def sem(t, name):
        key = names.setdefault(name, len(names))
        return rsem.at[t, key]

    def send(t, to, piece, name):
        copy = pltpu.make_async_remote_copy(
            src_ref=piece, dst_ref=piece, send_sem=ssem.at[t, n_sent[t]], recv_sem=sem(t, name),
            device_id={"dp": dev[to]}, device_id_type=MESH,
        )
        n_sent[t] += 1
        copy.start()
        sent.append(copy)

    def recv(t, piece, name):
        pltpu.make_async_copy(piece, piece, sem(t, name)).wait()

    def s0(t):
        own_y, own_x = ypiece(t, x, y), xpiece(t, x, y)
        send(t, "x+", own_x, "rx+")
        send(t, "x-", own_x, "rx-")
        send(t, "y+", own_y, "ry+1")
        send(t, "y-", own_y, "ry-1")
        send(t, "x+", own_y, "gx+")
        send(t, "x-", own_y, "gx-")
        send(t, "p", weights[t].at[x, y, c], "p")

    def r1(t):
        for s, d in (("+", -1), ("-", 1)):
            piece = xpiece(t, xs(d), y)
            recv(t, piece, "rx" + s)
            if s == "+-"[t]:
                send(t, "x" + s, piece, "rx2")
            send(t, "p", piece, "p")

    def r2(t):
        piece = xpiece(t, xs(2), y)
        recv(t, piece, "rx2")
        send(t, "p", piece, "p")

    def q0(t):
        for h in (0, 1):
            for s in "+-":
                send(t, "y" + s, xrow(t, y, h), f"qy{s}1{h}")

    def yphase(t, d):
        for s, m in (("+", -1), ("-", 1)):
            piece = ypiece(t, x, ys(m * d))
            recv(t, piece, f"ry{s}{d}")
            if d < 3:
                send(t, "y" + s, piece, f"ry{s}{d + 1}")
            else:
                h = "+-".index(s)
                send(t, "y" + s, yhalf(t, x, ys(m * d), h), f"ry{s}4")
            send(t, "p", piece, "p")

    def y4(t):
        for h, s in enumerate("+-"):
            recv(t, yhalf(t, x, ys(4), h), f"ry{s}4")
        send(t, "p", ypiece(t, x, ys(4)), "p")

    def xsend(t, *ds):
        for d in ds:
            for s in "+-":
                send(t, "x" + s, ypiece(t, x, ys(d)), "gx" + s)

    def qphase(t, d):
        for h in (0, 1):
            for s, m in (("+", -1), ("-", 1)):
                piece = xrow(t, ys(m * d), h)
                recv(t, piece, f"qy{s}{d}{h}")
                if d < 3 or h == "+-".index(s):
                    send(t, "y" + s, piece, f"qy{s}{d + 1}{h}")
                send(t, "p", piece, "p")

    def q4(t):
        for h, s in enumerate("+-"):
            piece = xrow(t, ys(4), h)
            recv(t, piece, f"qy{s}4{h}")
            send(t, "p", piece, "p")

    def g1(t):
        for h, (s, d) in enumerate((("+", -1), ("-", 1))):
            recv(t, ycol(t, xs(d)), "gx" + s)
            send(t, "x" + s, ycolhalf(t, xs(d), h), f"gx2{s}")
            send(t, "p", ycol(t, xs(d)), "p")

    def g2(t):
        for h, s in enumerate("+-"):
            piece = ycolhalf(t, xs(2), h)
            recv(t, piece, f"gx2{s}")
            send(t, "p", piece, "p")

    def pwait(t):
        recv(t, weights[t].at[:, :, 1 - c], "p")

    bins, width = cap_v.shape
    rows = img_v.shape[0]
    n_slots = out_buf.shape[0] * out_buf.shape[1]
    slot = out_buf.shape[1]

    def routing():
        owner = owner_ref[...]
        onehot_b = owner == lax.broadcasted_iota(jnp.int32, (bins, N_DP), 1)
        onehot = onehot_b.astype(F32)
        tri = (
            lax.broadcasted_iota(jnp.int32, (bins, bins), 1)
            < lax.broadcasted_iota(jnp.int32, (bins, bins), 0)
        ).astype(F32)
        before = jnp.dot(tri.astype(BF16), onehot.astype(BF16), preferred_element_type=F32)
        position = jnp.sum(before * onehot, axis=1, keepdims=True)
        target = owner * slot + position.astype(jnp.int32)
        picks[...] = (target == lax.broadcasted_iota(jnp.int32, (bins, n_slots), 1)).astype(F32).astype(BF16)
        counts = lax.dot_general(
            onehot.astype(BF16), jnp.ones((bins, 128), BF16), (((0,), (0,)), ((), ())),
            preferred_element_type=F32,
        )
        counts_out[...] = counts.reshape(N_DP, 1, 128)

    def split_mods():
        loads[2].wait()

        @pl.loop(0, width // 512)
        def _(i):
            cols = pl.ds(pl.multiple_of(i * 512, 512), 512)
            for j in (0, 1):
                value = cmod_v[:, j, cols]
                high = value.astype(BF16)
                rest = value - high.astype(F32)
                mid = rest.astype(BF16)
                low = (rest - mid.astype(F32)).astype(BF16)
                mod3[j, 0:N_DP, cols] = high
                mod3[j, N_DP : 2 * N_DP, cols] = mid
                mod3[j, 2 * N_DP :, cols] = low

    def row_mods():
        onehot = (owner_ref[...] == (lax.broadcasted_iota(jnp.int32, (bins, 3 * N_DP), 1) % N_DP)).astype(F32).astype(BF16)

        @pl.loop(0, width // 512)
        def _(i):
            cols = pl.ds(pl.multiple_of(i * 512, 512), 512)
            for j in (0, 1):
                modrow[j, :, cols] = jnp.dot(onehot, mod3[j, :, cols], preferred_element_type=F32)

    def norm(values):
        mean = jnp.mean(values, axis=-1, keepdims=True)
        values = values - mean
        var = jnp.mean(values * values, axis=-1, keepdims=True)
        return values * lax.rsqrt(var + 1e-06)

    def ln_txt(lo, n):
        @pl.loop(lo, lo + n)
        def _(i):
            r = pl.ds(pl.multiple_of(i * 16, 16), 16)
            values = norm(cap_v[r, :].astype(F32))
            txt_in[r, :] = (values * (1.0 + modrow[1, r, :]) + modrow[0, r, :]).astype(BF16)

    def ln_img(lo, n):
        @pl.loop(lo, lo + n)
        def _(i):
            r = pl.ds(pl.multiple_of(i * 16, 16), 16)
            values = norm(img_v[r, :].astype(F32))
            img_in[r, :] = (values * (1.0 + imod_ref[0, 1:2, :]) + imod_ref[0, 0:1, :]).astype(BF16)

    def project(left, t, p, gain_ref, n):
        total = None
        for xx in range(NX):
            w = weights[t][xx, :, :, p, :, :].reshape(width // NX, 256)
            part = jnp.dot(left[:, xx * (width // NX) : (xx + 1) * (width // NX)], w, preferred_element_type=F32)
            total = part if total is None else total + part
        if p == 2:
            return total.astype(BF16)
        heads = []
        for h in range(256 // HD):
            v = total[:, h * HD : (h + 1) * HD]
            v = v * lax.rsqrt(jnp.mean(v * v, axis=-1, keepdims=True) + 1e-06) * gain_ref[p : p + 1, :]
            heads.append(v)
        return jnp.concatenate(heads, axis=1).astype(BF16)

    def attend(blk, n):
        r = pl.ds(pl.multiple_of(blk * n, n), n)
        outs = []
        for h in range(256 // HD):
            lanes = slice(h * HD, (h + 1) * HD)
            s = lax.dot_general(
                qkv[0, r, lanes], qkv[1, :, lanes], (((1,), (1,)), ((), ())), preferred_element_type=F32
            )
            s = s + bias[0:1, :]
            top = jnp.max(s, axis=-1, keepdims=True)
            e = jnp.exp2((s - top) * (math.log2(math.e) / math.sqrt(HD)))
            e = e * (1.0 / jnp.sum(e, axis=-1, keepdims=True))
            outs.append(jnp.dot(e.astype(BF16), qkv[2, :, lanes], preferred_element_type=F32))
        return jnp.concatenate(outs, axis=1)

    def everyone(src, dst, k):
        own = pltpu.make_async_copy(src.at[dp], dst.at[dp], loc_sem.at[5 + k])
        own.start()

        @pl.loop(1, N_DP)
        def _(i):
            d = (dp + i) % N_DP
            pltpu.make_async_remote_copy(
                src_ref=src.at[d], dst_ref=dst.at[dp], send_sem=asem.at[0, k], recv_sem=asem.at[1, k],
                device_id={"dp": d}, device_id_type=MESH,
            ).start()

        def arrived():
            own.wait()
            pltpu.make_async_copy(dst.at[0 : N_DP - 1], dst.at[0 : N_DP - 1], asem.at[1, k]).wait()

        def left():
            pltpu.make_async_copy(src.at[0 : N_DP - 1], src.at[0 : N_DP - 1], asem.at[0, k]).wait()

        return arrived, left

    T, I = 0, 1
    loads[0].wait()
    loads[1].wait()
    pl.semaphore_wait(barrier, len(dev))
    s0(T)
    s0(I)
    routing()
    split_mods()
    r1(T)
    yphase(T, 1)
    xsend(T, -1, 1)
    yphase(I, 1)
    r1(I)
    r2(T)
    q0(T)
    row_mods()
    yphase(T, 2)
    xsend(T, -2, 2)
    xsend(I, -1, 1)
    r2(I)
    yphase(I, 2)
    loads[3].wait()
    ln_txt(0, 4)
    yphase(T, 3)
    xsend(T, -3, 3)
    qphase(T, 1)
    y4(T)
    xsend(T, 4)
    ln_txt(4, 4)
    yphase(I, 3)
    qphase(T, 2)
    ln_txt(8, 4)
    y4(I)
    q0(I)
    qphase(T, 3)
    ln_txt(12, 4)
    loads[4].wait()
    ln_img(0, 4)
    g1(T)
    xsend(I, -2, 2, -3, 3, 4)
    ln_img(4, 4)
    q4(T)
    g2(T)
    ln_img(8, 4)
    qphase(I, 1)
    pwait(T)
    counts_done, counts_left = everyone(counts_out, counts_in, 0)
    for p in range(3):
        payload[:, p * 256 : (p + 1) * 256] = project(txt_in, T, p, tgain_ref, bins)
        if p < 2:
            qphase(I, p + 2)
    for p in range(3):
        cols = slice(p * 256, (p + 1) * 256)
        routed = lax.dot_general(
            picks[...], payload[:, cols], (((0,), (0,)), ((), ())), preferred_element_type=F32
        )
        out_buf[:, :, cols] = routed.reshape(N_DP, slot, 256).astype(BF16)
    rows_done, rows_left = everyone(out_buf, in_buf, 1)
    q4(I)
    g1(I)
    ln_img(12, 20)
    g2(I)
    pwait(I)
    for p in range(3):
        qkv[p, n_slots:, :] = project(img_in, I, p, igain_ref, rows)
    counts_done()
    filled = counts_in[...].reshape(N_DP, 128)
    filled = jnp.concatenate([filled] * (n_slots // 128), axis=1)
    lane = lax.broadcasted_iota(jnp.int32, (N_DP, n_slots), 1)
    mine = lane // slot == lax.broadcasted_iota(jnp.int32, (N_DP, n_slots), 0)
    filled = jnp.sum(jnp.where(mine, filled, 0.0), axis=0, keepdims=True)
    place = (lax.broadcasted_iota(jnp.int32, (1, n_slots), 1) % slot).astype(F32)
    bias[0:1, 0:n_slots] = jnp.where(place < filled, 0.0, -jnp.inf)
    bias[0:1, n_slots:] = jnp.zeros((1, rows), F32)
    rows_done()
    for p in range(3):
        arrived = in_buf[:, :, p * 256 : (p + 1) * 256].astype(F32)
        qkv[p, 0:n_slots, :] = arrived.reshape(n_slots, 256).astype(BF16)
    n = 256

    @pl.loop(0, n_slots // n)
    def _(b):
        part = n // slot
        ret_out[pl.ds(b * part, part)] = attend(b, n).reshape(part, slot, 256).astype(BF16)

    back_done, back_left = everyone(ret_out, ret_in, 2)

    @pl.loop(0, rows // n)
    def _(b):
        oimg_ref[pl.ds(pl.multiple_of(b * n, n), n), :] = attend(n_slots // n + b, n).astype(BF16)

    back_done()
    returned = ret_in[...].astype(F32).reshape(n_slots, 256).astype(BF16)
    ocap_ref[...] = jnp.dot(picks[...], returned, preferred_element_type=F32).astype(BF16)
    for copy in sent:
        copy.wait_send()
    for left in (counts_left, rows_left, back_left):
        left()


def body(image_rows, image_mod, caption_rows, caption_mod, row_owner, w_img, w_txt, img_gain, txt_gain):
    rows, width = image_rows.shape
    bins = caption_rows.shape[0]
    slot = 2 * bins // N_DP
    n_slots = N_DP * slot
    depth, _, cols = w_img.shape
    w_img, w_txt = (jnp.transpose(w, (1, 0, 2)) for w in (w_img, w_txt))
    vmem = pl.BlockSpec(memory_space=pltpu.VMEM)
    hbm = pl.BlockSpec(memory_space=pl.ANY)
    return pl.pallas_call(
        kernel,
        out_shape=(
            jax.ShapeDtypeStruct((rows, cols), BF16),
            jax.ShapeDtypeStruct((bins, cols), BF16),
        ),
        in_specs=[hbm, vmem, hbm, hbm, vmem, hbm, hbm, vmem, vmem],
        out_specs=(vmem, vmem),
        scratch_shapes=[
            pltpu.VMEM((rows, width), BF16),
            pltpu.VMEM((bins, width), BF16),
            pltpu.VMEM((N_DP, 2, width), F32),
            pltpu.VMEM((2, 3 * N_DP, width), BF16),
            pltpu.VMEM((2, bins, width), F32),
            pltpu.VMEM((rows, width), BF16),
            pltpu.VMEM((bins, width), BF16),
            pltpu.VMEM((NX, NY, NC, 3, depth, cols), BF16),
            pltpu.VMEM((NX, NY, NC, 3, depth, cols), BF16),
            pltpu.VMEM((bins, n_slots), BF16),
            pltpu.VMEM((N_DP, 1, 128), F32),
            pltpu.VMEM((N_DP, 1, 128), F32),
            pltpu.VMEM((8, 128), F32),
            pltpu.VMEM((bins, 3 * cols), BF16),
            pltpu.VMEM((N_DP, slot, 3 * cols), BF16),
            pltpu.VMEM((N_DP, slot, 3 * cols), BF16),
            pltpu.VMEM((3, n_slots + rows, cols), BF16),
            pltpu.VMEM((N_DP, slot, cols), BF16),
            pltpu.VMEM((N_DP, slot, cols), BF16),
            pltpu.VMEM((8, n_slots + rows), F32),
            pltpu.SemaphoreType.DMA((8,)),
            pltpu.SemaphoreType.DMA((2, 32)),
            pltpu.SemaphoreType.DMA((2, 80)),
            pltpu.SemaphoreType.DMA((2, 3)),
        ],
        compiler_params=pltpu.CompilerParams(
            collective_id=0, has_side_effects=True, vmem_limit_bytes=60 * 1024 * 1024
        ),
        name="block",
    )(image_rows, image_mod, caption_rows, caption_mod, row_owner, w_img, w_txt, img_gain, txt_gain)


def solution(mesh):
    in_specs = (
        P("dp", None),
        P("dp", None, None),
        P("dp", None),
        P(),
        P("dp", None),
        P("dp", None, "tensor"),
        P("dp", None, "tensor"),
        P(),
        P(),
    )
    out_specs = (P("dp", "tensor"), P("dp", "tensor"))
    return jax.shard_map(body, mesh=mesh, in_specs=in_specs, out_specs=out_specs, check_vma=False)
```

time: 257 us -> 96.7 us (0.38)
  waiting for transfers between devices: 151 us -> 0 us
  Pallas kernels: 0 us -> 91.1 us
  starting transfers between devices: 27.3 us -> 0 us
  matrix products: 25.4 us -> 0 us
  local copies, waits for them, and re-layouts: 30.1 us -> 4.71 us
  between operations: 14.4 us -> 0.64 us
  other arithmetic: 8.79 us -> 0 us
    all_gather x2 -> x0, waiting for transfers between devices: 138 us -> none  [the longest x1 70 us: body(): lax.all_gather(w_img_qkv, 'dp', axis=0, tiled=True)]
    pallas_call x0 -> x1, Pallas kernels: none -> 91.1 us  [body(): pl.pallas_call(kernel, out_shape=(jax.ShapeDtypeStruct((rows, cols), BF16...]
    all_to_all x3 -> x0, starting transfers between devices: 27.2 us -> none  [the longest x1 14.5 us: body(): lax.all_to_all(present, 'dp', split_axis=0, concat_axis=0, tiled=True)]
    dot_general x4 -> x0, matrix products: 20.4 us -> none  [the longest x2 11.6 us: add_rows(): jnp.dot(left, piece.reshape(piece.shape[0], -1), preferred_element_type=j...]
    all_gather x2 -> x0, local copies, waits for them, and re-layouts: 13.3 us -> none  [the longest x1 6.63 us: body(): lax.all_gather(w_txt_qkv, 'dp', axis=0, tiled=True)]
    all_to_all x3 -> x0, waiting for transfers between devices: 11.1 us -> none  [the longest x1 11.1 us: body(): lax.all_to_all(caption_back, 'dp', split_axis=0, concat_axis=0, tiled=True)]
    scatter x2 -> x0, local copies, waits for them, and re-layouts: 5.2 us -> none  [the longest x1 3.04 us: body(): outgoing = jnp.zeros((n_dp * slot, 3 * cols_dev), jnp.bfloat16).at[target...]
    sub x1 -> x0, matrix products: 4.95 us -> none  [body(): weights = jax.nn.softmax(scores, axis=-1).astype(jnp.bfloat16)]
  transfers between devices with their start and end apart: 5 -> 0, of which waited for: 3 -> 0; matrix products, arithmetic and copies ran while one was open for 19% -> 0% of each run, Pallas kernels for 0% -> 0%
where the time goes in v1:
time: 96.7 us; the launch traced here: 96.5 us
  Pallas kernels  91.1 us (94%)
  local copies, waits for them, and re-layouts  4.71 us (5%)
    pallas_call x1, Pallas kernels, body(): pl.pallas_call(kernel, out_shape=(jax.ShapeDtypeStruct((rows, cols), BF16...  91.1 us
    unnamed x3, local copies, waits for them, and re-layouts  4.71 us

profile of v1, /device:TPU:1, one launch (start us, length us, event | category | flops | bytes accessed | tf_op | source)
XLA Modules:
  0.0 96.5 jit_solution(3509836344411126076)
XLA Ops:
  0.6 1.5 %copy.11.owner_ref = s32[256,1]{1,0:T(8,128)} copy(s32[256,1]{0,1:T(1,128)} %param.13) | data formatting | bytes 2048 | tf_op args[4]
  2.1 91.1 %block.1 = (bf16[512,256]{1,0:T(8,128)(2,1)}, bf16[256,256]{1,0:T(8,128)(2,1)}) custom-call(bf16[512,3072]{1,0:T(8,128)(2,1)} %img_hbm.1, f32[1,2,3072]{2,1,0:T(2,128)} %imod_ref.1, bf16[256,3072]{1,0:T(8,128)(2,1)} %cap_hbm.1, f32[64,2,3072]{2,1,0:T(2,128)} %cmod_hbm.1, s32[256,1]{1,0:T(8,128)} %copy.11.owner_ref, bf16[3,48,256]{2,1,0:T(8,128)(2,1)} %bitcast.2, ...), custom_call_target="tpu_custom_call" | custom-call | tf_op jit(solution)/shard_map/block/pallas_call | solution.py:403
  93.2 1.7 %copy.14 = bf16[512,256]{1,0:T(8,128)(2,1)} copy(bf16[512,256]{1,0:T(8,128)(2,1)} %get-tuple-element.4) | data formatting | bytes 524288
  94.9 1.6 %copy.15 = bf16[256,256]{1,0:T(8,128)(2,1)} copy(bf16[256,256]{1,0:T(8,128)(2,1)} %get-tuple-element.5) | data formatting | bytes 262144

commit v2 on v0

v2 whole, which is shorter than its diff:
```python
import math

import jax
import jax.numpy as jnp
from jax import lax
from jax.experimental import pallas as pl
from jax.experimental.pallas import tpu as pltpu
from jax.sharding import PartitionSpec as P

MESH = pl.DeviceIdType.MESH
HD = 128
NX, NY, NC = 4, 8, 2
N_DP = NX * NY * NC
F32 = jnp.float32
BF16 = jnp.bfloat16
T, I = 0, 1

ORDER = (
    ("s0", 0), ("s0", 1), ("route", 1), ("split", 8), ("rx", 0, "+"), ("rx", 0, "-"), ("split", 3), ("ry", 0, "+", 1),
    ("ry", 0, "-", 1), ("split", 1), ("mods", 2), ("gx", 0, "+", 0), ("gx", 0, "-", 0), ("qy", 0, 0, "+", 1),
    ("qy", 0, 0, "-", 1), ("mods", 10), ("rx", 1, "-"), ("gx", 1, "-", 0), ("lnt", 2), ("rx2", 0), ("qy", 0, -1, "+", 1),
    ("qy", 0, -1, "-", 1), ("lnt", 2), ("qy", 0, 1, "+", 1), ("qy", 0, 1, "-", 1), ("gx", 0, "-", -1), ("lnt", 2),
    ("gx", 0, "+", -1), ("lnt", 2), ("ry", 0, "+", 2), ("ry", 0, "-", 2), ("gx", 0, "-", 1), ("lnt", 2), ("gx", 0, "+", 1),
    ("qy", 0, 0, "+", 2), ("qy", 0, 0, "-", 2), ("lnt", 4), ("qy", 0, 2, "+", 1), ("qy", 0, 2, "-", 1), ("gx2", 0, "+", 0),
    ("lnt", 2), ("qy", 0, -1, "+", 2), ("qy", 0, -1, "-", 2), ("lni", 2), ("qy", 0, 1, "+", 2), ("qy", 0, 1, "-", 2),
    ("gx", 0, "-", -2), ("gx2", 0, "+", -1), ("gx", 1, "+", 0), ("lni", 4), ("ry", 0, "+", 3), ("ry", 0, "-", 3),
    ("gx", 0, "+", -2), ("gx", 0, "-", 2), ("lni", 2), ("qy", 0, 0, "+", 3), ("qy", 0, 0, "-", 3), ("qy", 1, 0, "-", 1),
    ("lni", 1), ("rx", 1, "+"), ("lni", 1), ("gx", 0, "+", 2), ("qy", 0, 2, "+", 2), ("qy", 0, 2, "-", 2),
    ("gx2", 0, "-", 1), ("lni", 1), ("qy", 0, -1, "+", 3), ("qy", 0, -1, "-", 3), ("lni", 2), ("qy", 0, 1, "+", 3),
    ("qy", 0, 1, "-", 3), ("gx2", 0, "-", -2), ("gx2", 1, "+", 0), ("lni", 2), ("ry", 0, "+", 4), ("ry", 0, "-", 4),
    ("qy", 1, 0, "+", 1), ("qy", 1, 1, "-", 1), ("lni", 1), ("rx2", 1), ("lni", 1), ("gx", 0, "+", -3), ("qy", 0, 0, "+", 4),
    ("gx", 0, "-", -3), ("lni", 1), ("qy", 1, 1, "+", 1), ("qy", 1, 0, "-", 2), ("lni", 2), ("gx", 0, "+", 3),
    ("qy", 0, 2, "+", 3), ("qy", 0, 2, "-", 3), ("gx", 0, "-", 3), ("qy", 1, -1, "+", 1), ("lni", 2), ("qy", 0, -1, "+", 4),
    ("qy", 0, 1, "-", 4), ("qy", 1, -1, "-", 1), ("lni", 2), ("gx2", 0, "+", 2), ("ry", 1, "+", 1), ("gx", 0, "-", 4),
    ("qy", 1, 1, "-", 2), ("lni", 1), ("qy", 1, 2, "-", 1), ("lni", 1), ("qy", 1, 0, "+", 2), ("lni", 1), ("gx", 0, "+", 4),
    ("qy", 1, 0, "-", 3), ("lni", 1), ("qy", 1, 2, "+", 1), ("lni", 1), ("qy", 0, 2, "-", 4), ("lni", 1), ("gx2", 0, "-", 3),
    ("ry", 1, "-", 1), ("qy", 1, 1, "+", 2), ("lni", 1), ("gx2", 0, "+", -3), ("lni", 1), ("qy", 1, -1, "+", 2),
    ("qy", 1, -1, "-", 2), ("ry", 1, "+", 2), ("gx", 1, "-", -1), ("qy", 1, 1, "-", 3), ("gx", 1, "+", -1),
    ("qy", 1, 2, "-", 2), ("qy", 1, 0, "+", 3), ("gx2", 0, "-", 4), ("qy", 1, 2, "+", 2), ("ry", 1, "-", 2),
    ("gx", 1, "+", 1), ("pw", 0), ("qy", 1, 1, "+", 3), ("gx", 1, "-", 1), ("qy", 1, -1, "+", 3), ("qy", 1, -1, "-", 3),
    ("proj", 0), ("gx", 1, "+", -2), ("qy", 1, 1, "-", 4), ("ry", 1, "+", 3), ("gx", 1, "-", -2), ("qy", 1, 2, "-", 3),
    ("send", 0, 0), ("send", 0, 1), ("qy", 1, 0, "+", 4), ("send", 0, 2), ("gx2", 1, "+", -1), ("qy", 1, 2, "+", 3),
    ("send", 0, 3), ("ry", 1, "-", 3), ("gx", 1, "-", 2), ("qy", 1, -1, "+", 4), ("send", 0, 4), ("gx", 1, "+", 2),
    ("ry", 1, "+", 4), ("qy", 1, 2, "-", 4), ("gx2", 1, "-", 1), ("send", 0, 5), ("gx", 1, "+", -3), ("send", 0, 6),
    ("gx", 1, "-", -3), ("gx2", 1, "-", -2), ("send", 0, 7), ("proj", 1), ("gx", 1, "+", 3), ("send", 1, 0),
    ("ry", 1, "-", 4), ("send", 1, 1), ("send", 1, 2), ("gx2", 1, "+", 2), ("send", 1, 3), ("gx", 1, "-", 3),
    ("gx2", 1, "+", -3), ("send", 1, 4), ("send", 1, 5), ("gx", 1, "-", 4), ("send", 1, 6), ("send", 1, 7), ("proj", 2),
    ("gx", 1, "+", 4), ("send", 2, 0), ("send", 2, 1), ("gx2", 1, "-", 3), ("send", 2, 2), ("send", 2, 3),
    ("gx2", 1, "-", 4), ("send", 2, 4), ("send", 2, 5), ("send", 2, 6), ("send", 2, 7), ("pw", 1),
)
ONWARD = {"+": (0, -1, 2, -3), "-": (1, -2, 3, 4)}


def sign(s):
    return 1 if s == "+" else -1


def kernel(
    img_hbm, imod_ref, cap_hbm, cmod_hbm, owner_ref, wimg_hbm, wtxt_hbm, igain_ref, tgain_ref,
    oimg_ref, ocap_ref,
    img_v, cap_v, cmod_v, mod3, modrow, img_in, txt_in, wt, wi, place_t, picks, onehot3, counts_out, counts_in,
    out_buf, in_buf, qkv, ret_out, ret_in, bias,
    loc_sem, rsem, ssem, asem,
):
    dp = lax.axis_index("dp")
    x, y, c = dp // (NY * NC), (dp // NC) % NY, dp % NC

    def at(xx, yy, cc):
        return (xx * NY + yy) * NC + cc

    def xs(d):
        return (x + d + NX) % NX

    def ys(d):
        return (y + d + NY) % NY

    dev = {
        "x+": at(xs(1), y, c), "x-": at(xs(-1), y, c),
        "y+": at(x, ys(1), c), "y-": at(x, ys(-1), c),
        "p": at(x, y, 1 - c),
    }
    weights = (wt, wi)

    loads = []
    for i, (src, dst) in enumerate((
        (wtxt_hbm, wt.at[x, y, c]), (wimg_hbm, wi.at[x, y, c]),
        (cmod_hbm, cmod_v), (cap_hbm, cap_v), (img_hbm, img_v),
    )):
        copy = pltpu.make_async_copy(src, dst, loc_sem.at[i])
        copy.start()
        loads.append(copy)

    barrier = pltpu.get_barrier_semaphore()
    for d in dev.values():
        pl.semaphore_signal(barrier, inc=1, device_id={"dp": d}, device_id_type=MESH)

    def ypiece(t, xx, yy):
        return weights[t].at[xx, yy, c, :, 16:48, :]

    def yhalf(t, xx, yy, s):
        lo = 16 if s == "+" else 32
        return weights[t].at[xx, yy, c, :, lo : lo + 16, :]

    def xpiece(t, xx, yy):
        return weights[t].at[xx, yy, c, :, 0:16, :]

    names = {}

    def sem(t, name):
        return rsem.at[t, names.setdefault(name, len(names))]

    def send(t, to, piece, name):
        kind = ("gx", "rx", "ry", "qy", "p").index("gx" if name[0] == "gx2" else "rx" if name[0] == "rx2" else name[0])
        pltpu.make_async_remote_copy(
            src_ref=piece, dst_ref=piece, send_sem=ssem.at[t, kind], recv_sem=sem(t, name),
            device_id={"dp": dev[to]}, device_id_type=MESH,
        ).start()

    def recv(t, piece, name):
        pltpu.make_async_copy(piece, piece, sem(t, name)).wait()

    def weights_sent(t):
        w = weights[t]
        for kind, piece in enumerate((
            w.at[0:2, :, 0], w.at[0, 0, 0], w.at[0:2, 0:7, 0, :, 0:16, :], w.at[:, 0:7, 0, :, 0:16, :], w.at[:, :, 0],
        )):
            pltpu.make_async_copy(piece, piece, ssem.at[t, kind]).wait()

    y4 = [0, 0]

    def s0(t):
        loads[t].wait()
        own_y, own_x = ypiece(t, x, y), xpiece(t, x, y)
        for s in "+-":
            send(t, "x" + s, own_x, ("rx", s))
            send(t, "y" + s, own_y, ("ry", s, 1))
            send(t, "x" + s, own_y, ("gx", s, 0))
        for s in "+-":
            send(t, "y" + s, own_x, ("qy", 0, s, 1))
        send(t, "p", weights[t].at[x, y, c], ("p",))

    def rx(t, s):
        piece = xpiece(t, xs(-sign(s)), y)
        recv(t, piece, ("rx", s))
        if s == "+-"[t]:
            send(t, "x" + s, piece, ("rx2",))
        for s2 in "+-":
            send(t, "y" + s2, piece, ("qy", -sign(s), s2, 1))
        send(t, "p", piece, ("p",))

    def rx2(t):
        piece = xpiece(t, xs(2), y)
        recv(t, piece, ("rx2",))
        for s2 in "+-":
            send(t, "y" + s2, piece, ("qy", 2, s2, 1))
        send(t, "p", piece, ("p",))

    def qy(t, j, s, d):
        piece = xpiece(t, xs(j), ys(-sign(s) * d))
        recv(t, piece, ("qy", j, s, d))
        if d < 3 or (d == 3 and (j in (0, -1)) == (s == "+")):
            send(t, "y" + s, piece, ("qy", j, s, d + 1))
        send(t, "p", piece, ("p",))

    def ry(t, s, d):
        if d == 4:
            piece = yhalf(t, x, ys(4), s)
            recv(t, piece, ("ry", s, 4))
            send(t, "p", piece, ("p",))
            y4[t] += 1
            if y4[t] == 2:
                for s2 in "+-":
                    send(t, "x" + s2, ypiece(t, x, ys(4)), ("gx", s2, 4))
            return
        dy = -sign(s) * d
        piece = ypiece(t, x, ys(dy))
        recv(t, piece, ("ry", s, d))
        if d < 3:
            send(t, "y" + s, piece, ("ry", s, d + 1))
        else:
            send(t, "y" + s, yhalf(t, x, ys(dy), s), ("ry", s, 4))
        for s2 in "+-":
            send(t, "x" + s2, piece, ("gx", s2, dy))
        send(t, "p", piece, ("p",))

    def gx(t, s, dy):
        piece = ypiece(t, xs(-sign(s)), ys(dy))
        recv(t, piece, ("gx", s, dy))
        if dy in ONWARD[s]:
            send(t, "x" + s, piece, ("gx2", s, dy))
        send(t, "p", piece, ("p",))

    def gx2(t, s, dy):
        piece = ypiece(t, xs(2), ys(dy))
        recv(t, piece, ("gx2", s, dy))
        send(t, "p", piece, ("p",))

    def pw(t):
        recv(t, weights[t].at[:, :, 1 - c], ("p",))

    bins, width = cap_v.shape
    rows = img_v.shape[0]
    _, _, slot, cols_dev = out_buf.shape
    n_slots = N_DP * slot
    iota = lambda shape, axis: lax.broadcasted_iota(jnp.int32, shape, axis)
    as_bf16 = lambda mask: mask.astype(F32).astype(BF16)

    def route():
        owner = owner_ref[...]
        own_t = as_bf16(owner == iota((N_DP, bins), 0))
        earlier = as_bf16(iota((bins, bins), 0) < iota((bins, bins), 1))
        before = jnp.dot(own_t, earlier, preferred_element_type=F32)
        position = jnp.sum(before * own_t.astype(F32), axis=0, keepdims=True)
        target = owner.astype(F32) * slot + position
        place_t[...] = as_bf16(iota((n_slots, bins), 0).astype(F32) == target)
        target_col = jnp.broadcast_to(target, (128, bins)).T[:, 0:1]
        picks[...] = as_bf16(iota((bins, n_slots), 1).astype(F32) == target_col)
        owner_col = jnp.broadcast_to(owner.astype(F32), (128, bins)).T[:, 0:1]
        onehot3[...] = as_bf16((iota((bins, 3 * N_DP), 1) % N_DP).astype(F32) == owner_col)
        counts = jnp.dot(own_t, jnp.ones((bins, 128), BF16), preferred_element_type=F32)
        counts_out[...] = counts.reshape(N_DP, 1, 128)

    tiles = width // 128

    def split(lo, n):
        @pl.loop(lo, lo + n)
        def _(k):
            lanes = pl.ds(pl.multiple_of(k * 128, 128), 128)
            for j in (0, 1):
                value = cmod_v[pl.ds(2 * k + j, N_DP, stride=2 * tiles), :]
                high = value.astype(BF16)
                rest = value - high.astype(F32)
                mid = rest.astype(BF16)
                low = (rest - mid.astype(F32)).astype(BF16)
                mod3[j, 0:N_DP, lanes] = high
                mod3[j, N_DP : 2 * N_DP, lanes] = mid
                mod3[j, 2 * N_DP :, lanes] = low

    def mods(lo, n):
        @pl.loop(lo, lo + n)
        def _(i):
            lanes = pl.ds(pl.multiple_of(i * 256, 256), 256)
            for j in (0, 1):
                modrow[j, :, lanes] = jnp.dot(onehot3[...], mod3[j, :, lanes], preferred_element_type=F32)

    def norm(values):
        values = values - jnp.mean(values, axis=-1, keepdims=True)
        var = jnp.mean(values * values, axis=-1, keepdims=True)
        return values * lax.rsqrt(var + 1e-06)

    def lnt(lo, n):
        @pl.loop(lo, lo + n)
        def _(i):
            r = pl.ds(pl.multiple_of(i * 16, 16), 16)
            values = norm(cap_v[r, :].astype(F32))
            txt_in[r, :] = (values * (1.0 + modrow[1, r, :]) + modrow[0, r, :]).astype(BF16)

    def lni(lo, n):
        @pl.loop(lo, lo + n)
        def _(i):
            r = pl.ds(pl.multiple_of(i * 16, 16), 16)
            values = norm(img_v[r, :].astype(F32))
            img_in[r, :] = (values * (1.0 + imod_ref[0, 1:2, :]) + imod_ref[0, 0:1, :]).astype(BF16)

    def project(left, t, p, gain_ref):
        total = None
        for xx in range(NX):
            w = weights[t][xx, :, :, p, :, :].reshape(width // NX, cols_dev)
            part = jnp.dot(left[:, xx * (width // NX) : (xx + 1) * (width // NX)], w, preferred_element_type=F32)
            total = part if total is None else total + part
        if p == 2:
            return total.astype(BF16)
        heads = []
        for h in range(cols_dev // HD):
            v = total[:, h * HD : (h + 1) * HD]
            v = v * lax.rsqrt(jnp.mean(v * v, axis=-1, keepdims=True) + 1e-06) * gain_ref[p : p + 1, :]
            heads.append(v)
        return jnp.concatenate(heads, axis=1).astype(BF16)

    def proj(p):
        routed = jnp.dot(place_t[...], project(txt_in, T, p, tgain_ref), preferred_element_type=F32)
        out_buf[p] = routed.reshape(N_DP, slot, cols_dev).astype(BF16)
        keep(out_buf.at[p], in_buf.at[p], 1 + p)

    kept = {}

    def keep(src, dst, k):
        kept[k] = (pltpu.make_async_copy(src.at[dp], dst.at[dp], loc_sem.at[5 + k]), src, dst)
        kept[k][0].start()

    def scatter(k, lo, hi):
        _, src, dst = kept[k]

        @pl.loop(lo, min(hi, N_DP - 1))
        def _(i):
            a, b, e = i // (NX * NC), (i // NC) % NX, i % NC
            dy = (4 - (a + 1) // 2) * (1 - 2 * ((a + 1) % 2))
            dx = (2 - (b + 1) // 2) * (1 - 2 * ((b + 1) % 2))
            d = at(xs(dx), ys(dy), (c + 1 + e) % NC)
            pltpu.make_async_remote_copy(
                src_ref=src.at[d], dst_ref=dst.at[dp], send_sem=asem.at[0, k], recv_sem=asem.at[1, k],
                device_id={"dp": d}, device_id_type=MESH,
            ).start()

    def arrived(k):
        own, _, dst = kept[k]
        own.wait()
        pltpu.make_async_copy(dst.at[0 : N_DP - 1], dst.at[0 : N_DP - 1], asem.at[1, k]).wait()

    def left(k):
        src = kept[k][1]
        pltpu.make_async_copy(src.at[0 : N_DP - 1], src.at[0 : N_DP - 1], asem.at[0, k]).wait()

    def attend(h, b, n):
        r = pl.ds(pl.multiple_of(b * n, n), n)
        lanes = slice(h * HD, (h + 1) * HD)
        s = lax.dot_general(
            qkv[0, r, lanes], qkv[1, :, lanes], (((1,), (1,)), ((), ())), preferred_element_type=F32
        )
        s = s + bias[0:1, :]
        top = jnp.max(s, axis=-1, keepdims=True)
        e = jnp.exp2((s - top) * (math.log2(math.e) / math.sqrt(HD)))
        e = e * (1.0 / jnp.sum(e, axis=-1, keepdims=True))
        return jnp.dot(e.astype(BF16), qkv[2, :, lanes], preferred_element_type=F32)

    pl.semaphore_wait(barrier, len(dev))
    moves = dict(s0=s0, rx=rx, rx2=rx2, qy=qy, ry=ry, gx=gx, gx2=gx2, pw=pw)
    work = dict(split=(split, 2, 2), mods=(mods, 1, None), lnt=(lnt, 1, 3), lni=(lni, 1, 4))
    done = dict.fromkeys(work, 0)
    for kind, *args in ORDER:
        if kind == "route":
            route()
        elif kind == "proj":
            proj(*args)
        elif kind == "send":
            p, batch = args
            scatter(1 + p, batch * NX * NC, (batch + 1) * NX * NC)
        elif kind in work:
            step, unit, load = work[kind]
            if load is not None and not done[kind]:
                loads[load].wait()
            step(done[kind] * unit, args[0] * unit)
            done[kind] += args[0]
        else:
            moves[kind](*args)
            if (kind, args[0]) == ("pw", T):
                keep(counts_out, counts_in, 0)
                scatter(0, 0, N_DP)
    for p in range(3):
        qkv[p, n_slots:, :] = project(img_in, I, p, igain_ref)
    arrived(0)
    filled = counts_in[...].reshape(N_DP, 128)
    filled = jnp.concatenate([filled] * (n_slots // 128), axis=1)
    mine = iota((N_DP, n_slots), 1) // slot == iota((N_DP, n_slots), 0)
    filled = jnp.sum(jnp.where(mine, filled, 0.0), axis=0, keepdims=True)
    place = (iota((1, n_slots), 1) % slot).astype(F32)
    bias[0:1, 0:n_slots] = jnp.where(place < filled, 0.0, -jnp.inf)
    bias[0:1, n_slots:] = jnp.zeros((1, rows), F32)
    for p in range(3):
        arrived(1 + p)
        qkv[p, 0:n_slots, :] = in_buf[p].astype(F32).reshape(n_slots, cols_dev).astype(BF16)
    n = 256
    part = n // slot
    heads = cols_dev // HD
    for h in range(heads):

        @pl.loop(0, n_slots // n)
        def _(b):
            ret_out[h, pl.ds(b * part, part)] = attend(h, b, n).reshape(part, slot, HD).astype(BF16)

        keep(ret_out.at[h], ret_in.at[h], 4 + h)
        scatter(4 + h, 0, N_DP)

    for h in range(heads):

        @pl.loop(0, rows // n)
        def _(b):
            lanes = slice(h * HD, (h + 1) * HD)
            oimg_ref[pl.ds(pl.multiple_of(b * n, n), n), lanes] = attend(h, n_slots // n + b, n).astype(BF16)

    weights_sent(T)
    weights_sent(I)
    for k in range(4 + heads):
        left(k)
    for h in range(heads):
        arrived(4 + h)
        returned = ret_in[h].astype(F32).reshape(n_slots, HD).astype(BF16)
        ocap_ref[:, h * HD : (h + 1) * HD] = jnp.dot(picks[...], returned, preferred_element_type=F32).astype(BF16)


def body(image_rows, image_mod, caption_rows, caption_mod, row_owner, w_img, w_txt, img_gain, txt_gain):
    rows, width = image_rows.shape
    bins = caption_rows.shape[0]
    slot = 2 * bins // N_DP
    n_slots = N_DP * slot
    depth, _, cols = w_img.shape
    w_img, w_txt = (jnp.transpose(w, (1, 0, 2)) for w in (w_img, w_txt))
    mods = caption_mod.reshape(N_DP, 2, width // 128, 128).transpose(0, 2, 1, 3).reshape(-1, 128)
    vmem = pl.BlockSpec(memory_space=pltpu.VMEM)
    hbm = pl.BlockSpec(memory_space=pl.ANY)
    return pl.pallas_call(
        kernel,
        out_shape=(
            jax.ShapeDtypeStruct((rows, cols), BF16),
            jax.ShapeDtypeStruct((bins, cols), BF16),
        ),
        in_specs=[hbm, vmem, hbm, hbm, vmem, hbm, hbm, vmem, vmem],
        out_specs=(vmem, vmem),
        scratch_shapes=[
            pltpu.VMEM((rows, width), BF16),
            pltpu.VMEM((bins, width), BF16),
            pltpu.VMEM(mods.shape, F32),
            pltpu.VMEM((2, 3 * N_DP, width), BF16),
            pltpu.VMEM((2, bins, width), F32),
            pltpu.VMEM((rows, width), BF16),
            pltpu.VMEM((bins, width), BF16),
            pltpu.VMEM((NX, NY, NC, 3, depth, cols), BF16),
            pltpu.VMEM((NX, NY, NC, 3, depth, cols), BF16),
            pltpu.VMEM((n_slots, bins), BF16),
            pltpu.VMEM((bins, n_slots), BF16),
            pltpu.VMEM((bins, 3 * N_DP), BF16),
            pltpu.VMEM((N_DP, 1, 128), F32),
            pltpu.VMEM((N_DP, 1, 128), F32),
            pltpu.VMEM((3, N_DP, slot, cols), BF16),
            pltpu.VMEM((3, N_DP, slot, cols), BF16),
            pltpu.VMEM((3, n_slots + rows, cols), BF16),
            pltpu.VMEM((cols // HD, N_DP, slot, HD), BF16),
            pltpu.VMEM((cols // HD, N_DP, slot, HD), BF16),
            pltpu.VMEM((8, n_slots + rows), F32),
            pltpu.SemaphoreType.DMA((16,)),
            pltpu.SemaphoreType.DMA((2, 64)),
            pltpu.SemaphoreType.DMA((2, 5)),
            pltpu.SemaphoreType.DMA((2, 6)),
        ],
        compiler_params=pltpu.CompilerParams(
            collective_id=0, has_side_effects=True, vmem_limit_bytes=60 * 1024 * 1024
        ),
        name="block",
    )(image_rows, image_mod, caption_rows, mods, row_owner.T, w_img, w_txt, img_gain, txt_gain)


def solution(mesh):
    in_specs = (
        P("dp", None),
        P("dp", None, None),
        P("dp", None),
        P(),
        P("dp", None),
        P("dp", None, "tensor"),
        P("dp", None, "tensor"),
        P(),
        P(),
    )
    out_specs = (P("dp", "tensor"), P("dp", "tensor"))
    return jax.shard_map(body, mesh=mesh, in_specs=in_specs, out_specs=out_specs, check_vma=False)
```

time: 257 us -> 82.8 us (0.32)
  waiting for transfers between devices: 151 us -> 0 us
  Pallas kernels: 0 us -> 78.7 us
  starting transfers between devices: 27.3 us -> 0 us
  local copies, waits for them, and re-layouts: 30.1 us -> 3.24 us
  matrix products: 25.4 us -> 0 us
  between operations: 14.4 us -> 0.64 us
  other arithmetic: 8.79 us -> 0 us
    all_gather x2 -> x0, waiting for transfers between devices: 138 us -> none  [the longest x1 70 us: body(): lax.all_gather(w_img_qkv, 'dp', axis=0, tiled=True)]
    pallas_call x0 -> x1, Pallas kernels: none -> 78.7 us  [body(): pl.pallas_call(kernel, out_shape=(jax.ShapeDtypeStruct((rows, cols), BF16...]
    all_to_all x3 -> x0, starting transfers between devices: 27.2 us -> none  [the longest x1 14.5 us: body(): lax.all_to_all(present, 'dp', split_axis=0, concat_axis=0, tiled=True)]
    dot_general x4 -> x0, matrix products: 20.4 us -> none  [the longest x2 11.6 us: add_rows(): jnp.dot(left, piece.reshape(piece.shape[0], -1), preferred_element_type=j...]
    all_gather x2 -> x0, local copies, waits for them, and re-layouts: 13.3 us -> none  [the longest x1 6.63 us: body(): lax.all_gather(w_txt_qkv, 'dp', axis=0, tiled=True)]
    all_to_all x3 -> x0, waiting for transfers between devices: 11.1 us -> none  [the longest x1 11.1 us: body(): lax.all_to_all(caption_back, 'dp', split_axis=0, concat_axis=0, tiled=True)]
    scatter x2 -> x0, local copies, waits for them, and re-layouts: 5.2 us -> none  [the longest x1 3.04 us: body(): outgoing = jnp.zeros((n_dp * slot, 3 * cols_dev), jnp.bfloat16).at[target...]
    sub x1 -> x0, matrix products: 4.95 us -> none  [body(): weights = jax.nn.softmax(scores, axis=-1).astype(jnp.bfloat16)]
  transfers between devices with their start and end apart: 5 -> 0, of which waited for: 3 -> 0; matrix products, arithmetic and copies ran while one was open for 19% -> 0% of each run, Pallas kernels for 0% -> 0%
where the time goes in v2:
time: 82.8 us; the launch traced here: 82.6 us
  Pallas kernels  78.7 us (95%)
  local copies, waits for them, and re-layouts  3.24 us (4%)
    pallas_call x1, Pallas kernels, body(): pl.pallas_call(kernel, out_shape=(jax.ShapeDtypeStruct((rows, cols), BF16...  78.7 us
    unnamed x2, local copies, waits for them, and re-layouts  3.24 us

profile of v2, /device:TPU:1, one launch (start us, length us, event | category | flops | bytes accessed | tf_op | source)
XLA Modules:
  0.0 82.6 jit_solution(2930789962262546100)
XLA Ops:
  0.6 78.7 %block.1 = (bf16[512,256]{1,0:T(8,128)(2,1)}, bf16[256,256]{1,0:T(8,128)(2,1)}) custom-call(bf16[512,3072]{1,0:T(8,128)(2,1)} %img_hbm.1, f32[1,2,3072]{2,1,0:T(2,128)} %imod_ref.1, bf16[256,3072]{1,0:T(8,128)(2,1)} %cap_hbm.1, f32[3072,128]{1,0:T(8,128)} %bitcast.8, s32[1,256]{1,0:T(1,128)} %bitcast.11, bf16[3,48,256]{2,1,0:T(8,128)(2,1)} %bitcast.9, ...), custom_call_target="tpu_custom_call" | custom-call | tf_op jit(solution)/shard_map/block/pallas_call | solution.py:401
  79.4 1.7 %copy.14 = bf16[512,256]{1,0:T(8,128)(2,1)} copy(bf16[512,256]{1,0:T(8,128)(2,1)} %get-tuple-element.4) | data formatting | bytes 524288
  81.0 1.6 %copy.15 = bf16[256,256]{1,0:T(8,128)(2,1)} copy(bf16[256,256]{1,0:T(8,128)(2,1)} %get-tuple-element.5) | data formatting | bytes 262144

commit v3 on v2

--- a/solution.py
+++ b/solution.py
@@ -109,10 +109,10 @@
     def sem(t, name):
         return rsem.at[t, names.setdefault(name, len(names))]
 
-    def send(t, to, piece, name):
+    def send(t, to, piece, name, source=None):
         kind = ("gx", "rx", "ry", "qy", "p").index("gx" if name[0] == "gx2" else "rx" if name[0] == "rx2" else name[0])
         pltpu.make_async_remote_copy(
-            src_ref=piece, dst_ref=piece, send_sem=ssem.at[t, kind], recv_sem=sem(t, name),
+            src_ref=piece if source is None else source, dst_ref=piece, send_sem=ssem.at[t, kind], recv_sem=sem(t, name),
             device_id={"dp": dev[to]}, device_id_type=MESH,
         ).start()
 
@@ -129,38 +129,39 @@
     y4 = [0, 0]
 
     def s0(t):
-        loads[t].wait()
+        shard = (wtxt_hbm, wimg_hbm)[t]
         own_y, own_x = ypiece(t, x, y), xpiece(t, x, y)
+        from_y, from_x = shard.at[:, 16:48, :], shard.at[:, 0:16, :]
         for s in "+-":
-            send(t, "x" + s, own_x, ("rx", s))
-            send(t, "y" + s, own_y, ("ry", s, 1))
-            send(t, "x" + s, own_y, ("gx", s, 0))
+            send(t, "x" + s, own_x, ("rx", s), from_x)
+            send(t, "y" + s, own_y, ("ry", s, 1), from_y)
+            send(t, "x" + s, own_y, ("gx", s, 0), from_y)
         for s in "+-":
-            send(t, "y" + s, own_x, ("qy", 0, s, 1))
-        send(t, "p", weights[t].at[x, y, c], ("p",))
+            send(t, "y" + s, own_x, ("qy", 0, s, 1), from_x)
+        send(t, "p", weights[t].at[x, y, c], ("p",), shard)
 
     def rx(t, s):
         piece = xpiece(t, xs(-sign(s)), y)
         recv(t, piece, ("rx", s))
+        send(t, "p", piece, ("p",))
         if s == "+-"[t]:
             send(t, "x" + s, piece, ("rx2",))
         for s2 in "+-":
             send(t, "y" + s2, piece, ("qy", -sign(s), s2, 1))
-        send(t, "p", piece, ("p",))
 
     def rx2(t):
         piece = xpiece(t, xs(2), y)
         recv(t, piece, ("rx2",))
+        send(t, "p", piece, ("p",))
         for s2 in "+-":
             send(t, "y" + s2, piece, ("qy", 2, s2, 1))
-        send(t, "p", piece, ("p",))
 
     def qy(t, j, s, d):
         piece = xpiece(t, xs(j), ys(-sign(s) * d))
         recv(t, piece, ("qy", j, s, d))
+        send(t, "p", piece, ("p",))
         if d < 3 or (d == 3 and (j in (0, -1)) == (s == "+")):
             send(t, "y" + s, piece, ("qy", j, s, d + 1))
-        send(t, "p", piece, ("p",))
 
     def ry(t, s, d):
         if d == 4:
@@ -175,20 +176,20 @@
         dy = -sign(s) * d
         piece = ypiece(t, x, ys(dy))
         recv(t, piece, ("ry", s, d))
+        send(t, "p", piece, ("p",))
         if d < 3:
             send(t, "y" + s, piece, ("ry", s, d + 1))
         else:
             send(t, "y" + s, yhalf(t, x, ys(dy), s), ("ry", s, 4))
         for s2 in "+-":
             send(t, "x" + s2, piece, ("gx", s2, dy))
-        send(t, "p", piece, ("p",))
 
     def gx(t, s, dy):
         piece = ypiece(t, xs(-sign(s)), ys(dy))
         recv(t, piece, ("gx", s, dy))
+        send(t, "p", piece, ("p",))
         if dy in ONWARD[s]:
             send(t, "x" + s, piece, ("gx2", s, dy))
-        send(t, "p", piece, ("p",))
 
     def gx2(t, s, dy):
         piece = ypiece(t, xs(2), ys(dy))
@@ -197,6 +198,7 @@
 
     def pw(t):
         recv(t, weights[t].at[:, :, 1 - c], ("p",))
+        loads[t].wait()
 
     bins, width = cap_v.shape
     rows = img_v.shape[0]
@@ -288,19 +290,24 @@
         kept[k] = (pltpu.make_async_copy(src.at[dp], dst.at[dp], loc_sem.at[5 + k]), src, dst)
         kept[k][0].start()
 
-    def scatter(k, lo, hi):
+    xnear = [xs(dx) * NY for dx in (2, 1, -1, 0)]
+    cnear = [1 - c, c]
+
+    def ring(k, yy, n):
         _, src, dst = kept[k]
-
-        @pl.loop(lo, min(hi, N_DP - 1))
-        def _(i):
-            a, b, e = i // (NX * NC), (i // NC) % NX, i % NC
-            dy = (4 - (a + 1) // 2) * (1 - 2 * ((a + 1) % 2))
-            dx = (2 - (b + 1) // 2) * (1 - 2 * ((b + 1) % 2))
-            d = at(xs(dx), ys(dy), (c + 1 + e) % NC)
+        for i in range(n):
+            d = (xnear[i // NC] + yy) * NC + cnear[i % NC]
             pltpu.make_async_remote_copy(
                 src_ref=src.at[d], dst_ref=dst.at[dp], send_sem=asem.at[0, k], recv_sem=asem.at[1, k],
                 device_id={"dp": d}, device_id_type=MESH,
             ).start()
+
+    def scatter(k):
+        @pl.loop(0, NY - 1)
+        def _(a):
+            ring(k, ys((4 - (a + 1) // 2) * (1 - 2 * ((a + 1) % 2))), NX * NC)
+
+        ring(k, y, NX * NC - 1)
 
     def arrived(k):
         own, _, dst = kept[k]
@@ -320,8 +327,8 @@
         s = s + bias[0:1, :]
         top = jnp.max(s, axis=-1, keepdims=True)
         e = jnp.exp2((s - top) * (math.log2(math.e) / math.sqrt(HD)))
-        e = e * (1.0 / jnp.sum(e, axis=-1, keepdims=True))
-        return jnp.dot(e.astype(BF16), qkv[2, :, lanes], preferred_element_type=F32)
+        out = jnp.dot(e.astype(BF16), qkv[2, :, lanes], preferred_element_type=F32)
+        return out * (1.0 / jnp.sum(e, axis=-1, keepdims=True))
 
     pl.semaphore_wait(barrier, len(dev))
     moves = dict(s0=s0, rx=rx, rx2=rx2, qy=qy, ry=ry, gx=gx, gx2=gx2, pw=pw)
@@ -334,7 +341,7 @@
             proj(*args)
         elif kind == "send":
             p, batch = args
-            scatter(1 + p, batch * NX * NC, (batch + 1) * NX * NC)
+            ring(1 + p, ys((4, 3, -3, 2, -2, 1, -1, 0)[batch]), NX * NC - (batch == NY - 1))
         elif kind in work:
             step, unit, load = work[kind]
             if load is not None and not done[kind]:
@@ -343,9 +350,8 @@
             done[kind] += args[0]
         else:
             moves[kind](*args)
-            if (kind, args[0]) == ("pw", T):
-                keep(counts_out, counts_in, 0)
-                scatter(0, 0, N_DP)
+    keep(counts_out, counts_in, 0)
+    scatter(0)
     for p in range(3):
         qkv[p, n_slots:, :] = project(img_in, I, p, igain_ref)
     arrived(0)
@@ -369,7 +375,7 @@
             ret_out[h, pl.ds(b * part, part)] = attend(h, b, n).reshape(part, slot, HD).astype(BF16)
 
         keep(ret_out.at[h], ret_in.at[h], 4 + h)
-        scatter(4 + h, 0, N_DP)
+        scatter(4 + h)
 
     for h in range(heads):
 
@@ -386,6 +392,11 @@
         arrived(4 + h)
         returned = ret_in[h].astype(F32).reshape(n_slots, HD).astype(BF16)
         ocap_ref[:, h * HD : (h + 1) * HD] = jnp.dot(picks[...], returned, preferred_element_type=F32).astype(BF16)
+
+
+def finish(image_ref, caption_ref, oimg_ref, ocap_ref):
+    oimg_ref[...] = image_ref[...]
+    ocap_ref[...] = caption_ref[...]
 
 
 def body(image_rows, image_mod, caption_rows, caption_mod, row_owner, w_img, w_txt, img_gain, txt_gain):
@@ -398,7 +409,7 @@
     mods = caption_mod.reshape(N_DP, 2, width // 128, 128).transpose(0, 2, 1, 3).reshape(-1, 128)
     vmem = pl.BlockSpec(memory_space=pltpu.VMEM)
     hbm = pl.BlockSpec(memory_space=pl.ANY)
-    return pl.pallas_call(
+    outs = pl.pallas_call(
         kernel,
         out_shape=(
             jax.ShapeDtypeStruct((rows, cols), BF16),
@@ -437,6 +448,14 @@
         ),
         name="block",
     )(image_rows, image_mod, caption_rows, mods, row_owner.T, w_img, w_txt, img_gain, txt_gain)
+    return pl.pallas_call(
+        finish,
+        out_shape=tuple(jax.ShapeDtypeStruct(o.shape, o.dtype) for o in outs),
+        in_specs=[vmem, vmem],
+        out_specs=(vmem, vmem),
+        compiler_params=pltpu.CompilerParams(vmem_limit_bytes=4 * 1024 * 1024),
+        name="finish",
+    )(*outs)
 
 
 def solution(mesh):

time: 82.8 us -> 80.2 us (0.969)
  local copies, waits for them, and re-layouts: 3.24 us -> 1.85 us
  Pallas kernels: 78.7 us -> 77.4 us
    pallas_call x1, Pallas kernels: 78.7 us -> 76.7 us  [body(): pl.pallas_call(kernel, out_shape=(jax.ShapeDtypeStruct((rows, cols), BF16...]
    unnamed x2 -> x4, local copies, waits for them, and re-layouts: 3.24 us -> 1.85 us
where the time goes in v3:
time: 80.2 us; the launch traced here: 79.9 us
  Pallas kernels  77.4 us (97%)
  local copies, waits for them, and re-layouts  1.85 us (2%)
    pallas_call x1, Pallas kernels, body(): pl.pallas_call(kernel, out_shape=(jax.ShapeDtypeStruct((rows, cols), BF16...  76.7 us
    unnamed x4, local copies, waits for them, and re-layouts  1.85 us

profile of v3, /device:TPU:1, one launch (start us, length us, event | category | flops | bytes accessed | tf_op | source)
XLA Modules:
  0.0 79.9 jit_solution(1277322812600745626)
XLA Ops:
  0.6 76.7 %block.1 = (bf16[512,256]{1,0:T(8,128)(2,1)}, bf16[256,256]{1,0:T(8,128)(2,1)}) custom-call(bf16[512,3072]{1,0:T(8,128)(2,1)} %img_hbm.1, f32[1,2,3072]{2,1,0:T(2,128)} %imod_ref.1, bf16[256,3072]{1,0:T(8,128)(2,1)} %cap_hbm.1, f32[3072,128]{1,0:T(8,128)} %bitcast.8, s32[1,256]{1,0:T(1,128)} %bitcast.11, bf16[3,48,256]{2,1,0:T(8,128)(2,1)} %bitcast.9, ...), custom_call_target="tpu_custom_call" | custom-call | tf_op jit(solution)/shard_map/block/pallas_call | solution.py:412
  77.3 0.0 copy-start
  77.3 0.9 %copy-done = bf16[512,256]{1,0:T(8,128)(2,1)S(1)} copy-done((bf16[512,256]{1,0:T(8,128)(2,1)S(1)}, bf16[512,256]{1,0:T(8,128)(2,1)}, u32[]{:S(2)}) %copy-start) | copy-done | bytes 262168
  78.2 0.0 copy-start.1
  78.2 0.9 %copy-done.1 = bf16[256,256]{1,0:T(8,128)(2,1)S(1)} copy-done((bf16[256,256]{1,0:T(8,128)(2,1)S(1)}, bf16[256,256]{1,0:T(8,128)(2,1)}, u32[]{:S(2)}) %copy-start.1) | copy-done | bytes 131096
  79.2 0.8 finish.1
Async XLA Ops:
  77.3 1.0 %copy-start = (bf16[512,256]{1,0:T(8,128)(2,1)S(1)}, bf16[512,256]{1,0:T(8,128)(2,1)}, u32[]{:S(2)}) copy-start(bf16[512,256]{1,0:T(8,128)(2,1)} %get-tuple-element.4.image_ref) | copy-start | bytes 786436
  78.2 0.9 %copy-start.1 = (bf16[256,256]{1,0:T(8,128)(2,1)S(1)}, bf16[256,256]{1,0:T(8,128)(2,1)}, u32[]{:S(2)}) copy-start(bf16[256,256]{1,0:T(8,128)(2,1)} %get-tuple-element.5.caption_ref) | copy-start | bytes 393220

commit v4 on v3

--- a/solution.py
+++ b/solution.py
@@ -16,37 +16,37 @@
 T, I = 0, 1
 
 ORDER = (
-    ("s0", 0), ("s0", 1), ("route", 1), ("split", 8), ("rx", 0, "+"), ("rx", 0, "-"), ("split", 3), ("ry", 0, "+", 1),
-    ("ry", 0, "-", 1), ("split", 1), ("mods", 2), ("gx", 0, "+", 0), ("gx", 0, "-", 0), ("qy", 0, 0, "+", 1),
-    ("qy", 0, 0, "-", 1), ("mods", 10), ("rx", 1, "-"), ("gx", 1, "-", 0), ("lnt", 2), ("rx2", 0), ("qy", 0, -1, "+", 1),
-    ("qy", 0, -1, "-", 1), ("lnt", 2), ("qy", 0, 1, "+", 1), ("qy", 0, 1, "-", 1), ("gx", 0, "-", -1), ("lnt", 2),
-    ("gx", 0, "+", -1), ("lnt", 2), ("ry", 0, "+", 2), ("ry", 0, "-", 2), ("gx", 0, "-", 1), ("lnt", 2), ("gx", 0, "+", 1),
-    ("qy", 0, 0, "+", 2), ("qy", 0, 0, "-", 2), ("lnt", 4), ("qy", 0, 2, "+", 1), ("qy", 0, 2, "-", 1), ("gx2", 0, "+", 0),
-    ("lnt", 2), ("qy", 0, -1, "+", 2), ("qy", 0, -1, "-", 2), ("lni", 2), ("qy", 0, 1, "+", 2), ("qy", 0, 1, "-", 2),
-    ("gx", 0, "-", -2), ("gx2", 0, "+", -1), ("gx", 1, "+", 0), ("lni", 4), ("ry", 0, "+", 3), ("ry", 0, "-", 3),
-    ("gx", 0, "+", -2), ("gx", 0, "-", 2), ("lni", 2), ("qy", 0, 0, "+", 3), ("qy", 0, 0, "-", 3), ("qy", 1, 0, "-", 1),
-    ("lni", 1), ("rx", 1, "+"), ("lni", 1), ("gx", 0, "+", 2), ("qy", 0, 2, "+", 2), ("qy", 0, 2, "-", 2),
-    ("gx2", 0, "-", 1), ("lni", 1), ("qy", 0, -1, "+", 3), ("qy", 0, -1, "-", 3), ("lni", 2), ("qy", 0, 1, "+", 3),
-    ("qy", 0, 1, "-", 3), ("gx2", 0, "-", -2), ("gx2", 1, "+", 0), ("lni", 2), ("ry", 0, "+", 4), ("ry", 0, "-", 4),
-    ("qy", 1, 0, "+", 1), ("qy", 1, 1, "-", 1), ("lni", 1), ("rx2", 1), ("lni", 1), ("gx", 0, "+", -3), ("qy", 0, 0, "+", 4),
-    ("gx", 0, "-", -3), ("lni", 1), ("qy", 1, 1, "+", 1), ("qy", 1, 0, "-", 2), ("lni", 2), ("gx", 0, "+", 3),
-    ("qy", 0, 2, "+", 3), ("qy", 0, 2, "-", 3), ("gx", 0, "-", 3), ("qy", 1, -1, "+", 1), ("lni", 2), ("qy", 0, -1, "+", 4),
-    ("qy", 0, 1, "-", 4), ("qy", 1, -1, "-", 1), ("lni", 2), ("gx2", 0, "+", 2), ("ry", 1, "+", 1), ("gx", 0, "-", 4),
-    ("qy", 1, 1, "-", 2), ("lni", 1), ("qy", 1, 2, "-", 1), ("lni", 1), ("qy", 1, 0, "+", 2), ("lni", 1), ("gx", 0, "+", 4),
-    ("qy", 1, 0, "-", 3), ("lni", 1), ("qy", 1, 2, "+", 1), ("lni", 1), ("qy", 0, 2, "-", 4), ("lni", 1), ("gx2", 0, "-", 3),
-    ("ry", 1, "-", 1), ("qy", 1, 1, "+", 2), ("lni", 1), ("gx2", 0, "+", -3), ("lni", 1), ("qy", 1, -1, "+", 2),
-    ("qy", 1, -1, "-", 2), ("ry", 1, "+", 2), ("gx", 1, "-", -1), ("qy", 1, 1, "-", 3), ("gx", 1, "+", -1),
-    ("qy", 1, 2, "-", 2), ("qy", 1, 0, "+", 3), ("gx2", 0, "-", 4), ("qy", 1, 2, "+", 2), ("ry", 1, "-", 2),
-    ("gx", 1, "+", 1), ("pw", 0), ("qy", 1, 1, "+", 3), ("gx", 1, "-", 1), ("qy", 1, -1, "+", 3), ("qy", 1, -1, "-", 3),
-    ("proj", 0), ("gx", 1, "+", -2), ("qy", 1, 1, "-", 4), ("ry", 1, "+", 3), ("gx", 1, "-", -2), ("qy", 1, 2, "-", 3),
-    ("send", 0, 0), ("send", 0, 1), ("qy", 1, 0, "+", 4), ("send", 0, 2), ("gx2", 1, "+", -1), ("qy", 1, 2, "+", 3),
-    ("send", 0, 3), ("ry", 1, "-", 3), ("gx", 1, "-", 2), ("qy", 1, -1, "+", 4), ("send", 0, 4), ("gx", 1, "+", 2),
-    ("ry", 1, "+", 4), ("qy", 1, 2, "-", 4), ("gx2", 1, "-", 1), ("send", 0, 5), ("gx", 1, "+", -3), ("send", 0, 6),
-    ("gx", 1, "-", -3), ("gx2", 1, "-", -2), ("send", 0, 7), ("proj", 1), ("gx", 1, "+", 3), ("send", 1, 0),
-    ("ry", 1, "-", 4), ("send", 1, 1), ("send", 1, 2), ("gx2", 1, "+", 2), ("send", 1, 3), ("gx", 1, "-", 3),
-    ("gx2", 1, "+", -3), ("send", 1, 4), ("send", 1, 5), ("gx", 1, "-", 4), ("send", 1, 6), ("send", 1, 7), ("proj", 2),
-    ("gx", 1, "+", 4), ("send", 2, 0), ("send", 2, 1), ("gx2", 1, "-", 3), ("send", 2, 2), ("send", 2, 3),
-    ("gx2", 1, "-", 4), ("send", 2, 4), ("send", 2, 5), ("send", 2, 6), ("send", 2, 7), ("pw", 1),
+    ("s0", 0), ("s0", 1), ("route", 1), ("split", 10), ("rx", 0, "+"), ("rx", 0, "-"), ("split", 2), ("mods", 1),
+    ("ry", 0, "+", 1), ("ry", 0, "-", 1), ("mods", 3), ("gx", 0, "+", 0), ("gx", 0, "-", 0), ("qy", 0, 0, "+", 1),
+    ("qy", 0, 0, "-", 1), ("mods", 3), ("rx", 1, "-"), ("mods", 5), ("lnt", 1), ("gx", 1, "-", 0), ("rx", 1, "+"),
+    ("lnt", 2), ("rx2", 0), ("qy", 0, -1, "+", 1), ("qy", 0, -1, "-", 1), ("gx", 1, "+", 0), ("lnt", 2),
+    ("qy", 0, 1, "+", 1), ("qy", 0, 1, "-", 1), ("gx", 0, "-", -1), ("lnt", 2), ("gx", 0, "+", -1), ("lnt", 2),
+    ("ry", 0, "+", 2), ("ry", 0, "-", 2), ("gx", 0, "-", 1), ("lnt", 2), ("gx", 0, "+", 1), ("qy", 0, 0, "+", 2),
+    ("qy", 0, 0, "-", 2), ("lnt", 4), ("gx2", 0, "+", 0), ("qy", 1, 0, "+", 1), ("qy", 1, 0, "-", 1), ("lnt", 1), ("lni", 1),
+    ("qy", 0, 2, "+", 1), ("qy", 0, 2, "-", 1), ("lni", 2), ("qy", 0, -1, "+", 2), ("qy", 0, -1, "-", 2), ("gx2", 1, "+", 0),
+    ("lni", 1), ("gx", 0, "-", -2), ("qy", 0, 1, "+", 2), ("qy", 0, 1, "-", 2), ("lni", 2), ("gx2", 0, "+", -1),
+    ("ry", 1, "+", 1), ("qy", 1, 1, "-", 1), ("lni", 2), ("ry", 0, "+", 3), ("ry", 0, "-", 3), ("gx", 0, "-", 2), ("lni", 2),
+    ("gx", 0, "+", -2), ("qy", 0, 0, "+", 3), ("qy", 0, 0, "-", 3), ("qy", 1, -1, "-", 1), ("lni", 2), ("gx2", 0, "-", 1),
+    ("qy", 1, 0, "-", 2), ("lni", 2), ("gx", 0, "+", 2), ("qy", 0, 2, "+", 2), ("qy", 0, 2, "-", 2), ("lni", 1),
+    ("gx2", 0, "-", -2), ("qy", 0, -1, "+", 3), ("qy", 0, -1, "-", 3), ("lni", 2), ("qy", 0, 1, "+", 3),
+    ("qy", 0, 1, "-", 3), ("ry", 1, "-", 1), ("qy", 1, 1, "+", 1), ("lni", 2), ("qy", 1, -1, "+", 1), ("gx", 1, "-", -1),
+    ("lni", 2), ("ry", 0, "-", 4), ("gx", 0, "+", -3), ("rx2", 1), ("lni", 2), ("ry", 0, "+", 4), ("gx", 0, "-", -3),
+    ("qy", 1, 0, "+", 2), ("qy", 1, 1, "-", 2), ("lni", 2), ("gx", 0, "+", 3), ("qy", 0, 0, "+", 4), ("qy", 1, -1, "-", 2),
+    ("lni", 1), ("gx", 0, "-", 3), ("qy", 0, 2, "+", 3), ("qy", 0, 2, "-", 3), ("lni", 2), ("qy", 0, -1, "+", 4),
+    ("qy", 0, 1, "-", 4), ("gx2", 0, "+", 2), ("gx", 1, "+", -1), ("qy", 1, 0, "-", 3), ("lni", 2), ("gx", 1, "-", 1),
+    ("qy", 1, 1, "+", 2), ("lni", 2), ("ry", 1, "+", 2), ("gx", 1, "+", 1), ("qy", 1, -1, "+", 2), ("gx", 0, "-", 4),
+    ("qy", 1, 2, "-", 1), ("qy", 1, 2, "+", 1), ("gx2", 0, "+", -3), ("qy", 1, 1, "-", 3), ("qy", 1, 0, "+", 3),
+    ("gx2", 0, "-", 3), ("ry", 1, "-", 2), ("qy", 1, -1, "-", 3), ("gx", 0, "+", 4), ("qy", 0, 2, "-", 4),
+    ("qy", 1, 1, "+", 3), ("gx2", 1, "-", 1), ("qy", 1, 2, "-", 2), ("gx2", 1, "+", -1), ("ry", 1, "+", 3),
+    ("qy", 1, 1, "-", 4), ("qy", 1, -1, "+", 3), ("gx", 1, "-", -2), ("gx", 1, "+", -2), ("qy", 1, 2, "+", 2),
+    ("gx2", 0, "-", 4), ("ry", 1, "-", 3), ("qy", 1, 0, "+", 4), ("gx", 1, "+", 2), ("qy", 1, 2, "-", 3), ("gx", 1, "-", 2),
+    ("ry", 1, "+", 4), ("pw", 0), ("proj", 0), ("qy", 1, -1, "+", 4), ("gx", 1, "+", -3), ("qy", 1, 2, "+", 3),
+    ("gx", 1, "-", -3), ("send", 0, 0), ("ry", 1, "-", 4), ("send", 0, 1), ("send", 0, 2), ("send", 0, 3), ("gx", 1, "+", 3),
+    ("gx2", 1, "-", -2), ("qy", 1, 2, "-", 4), ("send", 0, 4), ("gx2", 1, "+", 2), ("gx", 1, "-", 3), ("send", 0, 5),
+    ("gx2", 1, "+", -3), ("send", 0, 6), ("send", 0, 7), ("proj", 1), ("gx", 1, "-", 4), ("send", 1, 0), ("gx", 1, "+", 4),
+    ("gx2", 1, "-", 3), ("send", 1, 1), ("send", 1, 2), ("send", 1, 3), ("gx2", 1, "-", 4), ("send", 1, 4), ("send", 1, 5),
+    ("send", 1, 6), ("send", 1, 7), ("proj", 2), ("send", 2, 0), ("send", 2, 1), ("send", 2, 2), ("send", 2, 3),
+    ("send", 2, 4), ("send", 2, 5), ("send", 2, 6), ("send", 2, 7), ("pw", 1),
 )
 ONWARD = {"+": (0, -1, 2, -3), "-": (1, -2, 3, 4)}
 
@@ -453,7 +453,7 @@
         out_shape=tuple(jax.ShapeDtypeStruct(o.shape, o.dtype) for o in outs),
         in_specs=[vmem, vmem],
         out_specs=(vmem, vmem),
-        compiler_params=pltpu.CompilerParams(vmem_limit_bytes=4 * 1024 * 1024),
+        compiler_params=pltpu.CompilerParams(vmem_limit_bytes=60 * 1024 * 1024),
         name="finish",
     )(*outs)
 

time: 80.2 us -> 78.9 us (0.984)
  local copies, waits for them, and re-layouts: 1.85 us -> 0 us
    unnamed x4 -> x0, local copies, waits for them, and re-layouts: 1.85 us -> none
    pallas_call x1, Pallas kernels: 0.77 us -> 1.74 us  [body(): pl.pallas_call(finish, out_shape=tuple((jax.ShapeDtypeStruct(o.shape, o.d...]
where the time goes in v4:
time: 78.9 us; the launch traced here: 78.7 us
  Pallas kernels  78 us (99%)
    pallas_call x1, Pallas kernels, body(): pl.pallas_call(kernel, out_shape=(jax.ShapeDtypeStruct((rows, cols), BF16...  76.3 us
    pallas_call x1, Pallas kernels, body(): pl.pallas_call(finish, out_shape=tuple((jax.ShapeDtypeStruct(o.shape, o.d...  1.74 us

profile of v4, /device:TPU:1, one launch (start us, length us, event | category | flops | bytes accessed | tf_op | source)
XLA Modules:
  0.0 78.7 jit_solution(9753569525223411556)
XLA Ops:
  0.6 76.3 %block.1 = (bf16[512,256]{1,0:T(8,128)(2,1)}, bf16[256,256]{1,0:T(8,128)(2,1)}) custom-call(bf16[512,3072]{1,0:T(8,128)(2,1)} %img_hbm.1, f32[1,2,3072]{2,1,0:T(2,128)} %imod_ref.1, bf16[256,3072]{1,0:T(8,128)(2,1)} %cap_hbm.1, f32[3072,128]{1,0:T(8,128)} %bitcast.8, s32[1,256]{1,0:T(1,128)} %bitcast.11, bf16[3,48,256]{2,1,0:T(8,128)(2,1)} %bitcast.9, ...), custom_call_target="tpu_custom_call" | custom-call | tf_op jit(solution)/shard_map/block/pallas_call | solution.py:412
  76.9 1.7 %finish.1 = (bf16[512,256]{1,0:T(8,128)(2,1)}, bf16[256,256]{1,0:T(8,128)(2,1)}) custom-call(bf16[512,256]{1,0:T(8,128)(2,1)} %get-tuple-element.4.image_ref, bf16[256,256]{1,0:T(8,128)(2,1)} %get-tuple-element.5.caption_ref), custom_call_target="tpu_custom_call" | custom-call | tf_op jit(solution)/shard_map/finish/pallas_call | solution.py:451

commit v5 on v4

--- a/solution.py
+++ b/solution.py
@@ -338,6 +338,9 @@
         if kind == "route":
             route()
         elif kind == "proj":
+            if args == [1]:
+                keep(counts_out, counts_in, 0)
+                scatter(0)
             proj(*args)
         elif kind == "send":
             p, batch = args
@@ -350,8 +353,6 @@
             done[kind] += args[0]
         else:
             moves[kind](*args)
-    keep(counts_out, counts_in, 0)
-    scatter(0)
     for p in range(3):
         qkv[p, n_slots:, :] = project(img_in, I, p, igain_ref)
     arrived(0)
@@ -384,14 +385,14 @@
             lanes = slice(h * HD, (h + 1) * HD)
             oimg_ref[pl.ds(pl.multiple_of(b * n, n), n), lanes] = attend(h, n_slots // n + b, n).astype(BF16)
 
+    for h in range(heads):
+        arrived(4 + h)
+        returned = ret_in[h].astype(F32).reshape(n_slots, HD).astype(BF16)
+        ocap_ref[:, h * HD : (h + 1) * HD] = jnp.dot(picks[...], returned, preferred_element_type=F32).astype(BF16)
     weights_sent(T)
     weights_sent(I)
     for k in range(4 + heads):
         left(k)
-    for h in range(heads):
-        arrived(4 + h)
-        returned = ret_in[h].astype(F32).reshape(n_slots, HD).astype(BF16)
-        ocap_ref[:, h * HD : (h + 1) * HD] = jnp.dot(picks[...], returned, preferred_element_type=F32).astype(BF16)
 
 
 def finish(image_ref, caption_ref, oimg_ref, ocap_ref):

time: 78.9 us -> 78.3 us (level)
  no operation moved by 1% of the time
where the time goes in v5:
time: 78.3 us; the launch traced here: 78.1 us
  Pallas kernels  77.5 us (99%)
    pallas_call x1, Pallas kernels, body(): pl.pallas_call(kernel, out_shape=(jax.ShapeDtypeStruct((rows, cols), BF16...  75.7 us
    pallas_call x1, Pallas kernels, body(): pl.pallas_call(finish, out_shape=tuple((jax.ShapeDtypeStruct(o.shape, o.d...  1.74 us

profile of v5, /device:TPU:1, one launch (start us, length us, event | category | flops | bytes accessed | tf_op | source)
XLA Modules:
  0.0 78.1 jit_solution(10454139723251738838)
XLA Ops:
  0.6 75.7 %block.1 = (bf16[512,256]{1,0:T(8,128)(2,1)}, bf16[256,256]{1,0:T(8,128)(2,1)}) custom-call(bf16[512,3072]{1,0:T(8,128)(2,1)} %img_hbm.1, f32[1,2,3072]{2,1,0:T(2,128)} %imod_ref.1, bf16[256,3072]{1,0:T(8,128)(2,1)} %cap_hbm.1, f32[3072,128]{1,0:T(8,128)} %bitcast.8, s32[1,256]{1,0:T(1,128)} %bitcast.11, bf16[3,48,256]{2,1,0:T(8,128)(2,1)} %bitcast.9, ...), custom_call_target="tpu_custom_call" | custom-call | tf_op jit(solution)/shard_map/block/pallas_call | solution.py:413
  76.4 1.7 %finish.1 = (bf16[512,256]{1,0:T(8,128)(2,1)}, bf16[256,256]{1,0:T(8,128)(2,1)}) custom-call(bf16[512,256]{1,0:T(8,128)(2,1)} %get-tuple-element.4.image_ref, bf16[256,256]{1,0:T(8,128)(2,1)} %get-tuple-element.5.caption_ref), custom_call_target="tpu_custom_call" | custom-call | tf_op jit(solution)/shard_map/finish/pallas_call | solution.py:452
